TPU v7x, 32 devices: a whole 2x2x4 slice. The times are simulated.
32 devices in a mesh: dp: 16 (over z, x, core), tensor: 2 (over y).
Axes of the slice: x: 2, y: 2, z: 4, core: 2. Of those that a mesh axis runs over, the one named last changes fastest.
Arguments:
- tokens: bfloat16 [8192, 1024], P(('dp', 'tensor')), may hold values from -6 to 6
- cotangent: bfloat16 [8192, 1024], P(('dp', 'tensor')), may hold values from -6 to 6
- segments: int32 [16, 512], P('dp'), may hold values from 0 to 7, never falling along the last dimension, each value on 1 to 128 neighbouring positions
- ln_gain: float32 [1024], replicated, may hold values from 0.5 to 1.5
- ln_bias: float32 [1024], replicated, may hold values from -2 to 2
- w_qkv: bfloat16 [1024, 3072], P('dp', 'tensor'), may hold values from -0.1875 to 0.1875
- b_qkv: float32 [3072], P('tensor'), may hold values from -2 to 2
- w_dense: bfloat16 [1024, 1024], P('tensor', 'dp'), may hold values from -0.5 to 0.5
- b_dense: float32 [1024], replicated, may hold values from -2 to 2
- w_up: bfloat16 [1024, 4096], P('dp', 'tensor'), may hold values from -0.1875 to 0.1875
- b_up: float32 [4096], P('tensor'), may hold values from -2 to 2
- w_down: bfloat16 [4096, 1024], P('tensor', 'dp'), may hold values from -0.09375 to 0.09375
- b_down: float32 [1024], replicated, may hold values from -2 to 2
Outputs:
- output: bfloat16 [8192, 1024], P(('dp', 'tensor'))
- input_grad: float32 [8192, 1024], P(('dp', 'tensor'))
- ln_gain_grad: float32 [1024], replicated
- ln_bias_grad: float32 [1024], replicated
- qkv_grad: float32 [1024, 3072], P('dp', 'tensor')
- qkv_bias_grad: float32 [3072], P('tensor')
- dense_grad: float32 [1024, 1024], P('tensor', 'dp')
- dense_bias_grad: float32 [1024], replicated
- up_grad: float32 [1024, 4096], P('dp', 'tensor')
- up_bias_grad: float32 [4096], P('tensor')
- down_grad: float32 [4096, 1024], P('tensor', 'dp')
- down_bias_grad: float32 [1024], replicated
Inputs may be any that keep to these rules, and one draw needn't show every extreme that they name: `segments`: within each sequence the document numbers never fall, every number from 0 to 7 is used, each document has at least one token and some document has exactly 128 tokens.
All inputs are finite; a program needn't handle non-finite values.
Results may differ from a plain program's by a relative error of at most 0.0085.
Values may be sent and summed in bfloat16 or wider, within the bound.
A program may use at most 128 MiB of HBM per device.

v0:
```python
import functools

import jax
import jax.numpy as jnp
import numpy as np
from jax import lax
from jax.experimental import pallas as pl
from jax.experimental.pallas import tpu as pltpu
from jax.sharding import PartitionSpec as P

HEAD = 64
ROT = 16
NORM_EPS = 1e-05
ROTARY_BASE = 10000.0
MESH = pl.DeviceIdType.MESH
F32 = jnp.float32
BF16 = jnp.bfloat16


def dot(left, right, over_left, over_right):
    return lax.dot_general(
        left, right, (((over_left,), (over_right,)), ((), ())), preferred_element_type=F32
    )


def normalize(rows):
    centred = rows - jnp.mean(rows, axis=-1, keepdims=True)
    inverse = lax.rsqrt(jnp.mean(centred * centred, axis=-1, keepdims=True) + NORM_EPS)
    return centred * inverse, inverse


def kernel(
    sizes,
    tokens,
    cotangent,
    segments,
    gain,
    shift,
    w_qkv,
    b_qkv,
    w_dense,
    b_dense,
    w_up,
    b_up,
    w_down,
    b_down,
    output,
    input_grad,
    gain_grad,
    shift_grad,
    qkv_grad,
    qkv_bias,
    dense_grad,
    dense_bias,
    up_grad,
    up_bias,
    down_grad,
    wa_in,
    ba,
    cos_table,
    sin_table,
    docs,
    doc_column,
    wa,
    wu,
    wd,
    normed,
    grads,
    query,
    key,
    value,
    grad_out,
    attended,
    grad_z,
    key_sum,
    value_sum,
    active,
    slope,
    grad_u,
    core_in,
    turn_in,
    own_rows,
    own_a,
    own_u,
    own_d,
    xs_a,
    xs_u,
    xs_d,
    xr_a,
    xr_u,
    xr_d,
    zs_a,
    zs_u,
    zs_d,
    zr_a,
    zr_u,
    zr_d,
    fs_a,
    fs_u,
    fs_d,
    keep_a,
    fr_a,
    vec,
    vec_in,
    vec_t,
    vec_z,
    local_sem,
    core_sem,
    up_send,
    down_send,
    x_send,
    z_recv,
    x_recv,
    act_send,
    act_recv,
    pass_send,
    pass_recv,
    rx_send,
    rx_recv,
    rz_send,
    rz_recv,
    fin_send,
    fin_recv,
    half_send,
    half_recv,
    turn_send,
    turn_recv,
    vec_send,
    vec_recv,
    credit,
):
    nt, nz, na, nm, hp, length, R, r, pw = (
        sizes[k] for k in ("nt", "nz", "na", "nm", "hp", "length", "R", "r", "pw")
    )
    D = tokens.shape[1]
    half = D // 2
    chip = 2 * r
    partials = (grads, normed)
    wide = hp * HEAD
    units = nm * pw
    dp, t = lax.axis_index("dp"), lax.axis_index("tensor")
    z, x, c = dp // 4, (dp // 2) % 2, dp % 2

    def device(zz, xx, cc, tt):
        return (zz * 4 + xx * 2 + cc, tt)

    partner = device(z, x, 1 - c, t)
    across = device(z, 1 - x, c, t)

    def along(zz):
        return device(zz, x, c, t)

    def turned(tt):
        return device(z, x, c, tt)

    def other_z(k):
        return lax.rem(z + k, nz)

    def other_t(k):
        return lax.rem(t + k, nt)

    def copy(src, dst, send, recv, to):
        return pltpu.make_async_remote_copy(
            src_ref=src, dst_ref=dst, send_sem=send, recv_sem=recv, device_id=to, device_id_type=MESH
        )

    pieces = (
        [(wa, k) for k in range(na)] + [(wu, k) for k in range(nm)] + [(wd, k) for k in range(nm)]
    )
    A = list(range(na))
    U = list(range(na, na + nm))
    Dn = list(range(na + nm, na + 2 * nm))
    own_of = [own_a.at[k] for k in range(na)] + [own_u.at[k] for k in range(nm)] + [own_d.at[k] for k in range(nm)]
    xs_of = [xs_a.at[k] for k in range(na)] + [xs_u.at[k] for k in range(nm)] + [xs_d.at[k] for k in range(nm)]
    xr_of = [xr_a.at[k] for k in range(na)] + [xr_u.at[k] for k in range(nm)] + [xr_d.at[k] for k in range(nm)]
    zs_of = [zs_a.at[k] for k in range(na)] + [zs_u.at[k] for k in range(nm)] + [zs_d.at[k] for k in range(nm)]
    zr_of = [zr_a.at[k] for k in range(na)] + [zr_u.at[k] for k in range(nm)] + [zr_d.at[k] for k in range(nm)]
    fs_of = [fs_a.at[k] for k in range(na)] + [fs_u.at[k] for k in range(nm)] + [fs_d.at[k] for k in range(nm)]

    def chip_rows(xx, zz):
        return pl.ds(pl.multiple_of((xx * nz + zz) * chip, chip), chip)

    own_block = pl.ds(pl.multiple_of((x * nz + z) * chip + c * r, r), r)

    barrier = pltpu.get_barrier_semaphore()
    greeted = [partner, across] + [along(other_z(k)) for k in range(1, nz)] + [turned(other_t(k)) for k in range(1, nt)]
    for other in greeted:
        pl.semaphore_signal(barrier, inc=1, device_id=other, device_id_type=MESH)
    pl.semaphore_wait(barrier, len(greeted))

    def half_of(i, cc):
        if i in A:
            return wa_in.at[cc, i]
        if i in U:
            return w_up.at[:, pl.ds(pl.multiple_of(cc * units + (i - na) * pw, pw), pw)]
        return w_down.at[:, pl.ds(pl.multiple_of(cc * units + (i - na - nm) * pw, pw), pw)]

    def local_copy(i):
        ref, k = pieces[i]
        return pltpu.make_async_copy(half_of(i, c), ref.at[k, own_block], local_sem.at[i])

    def core_copy(i):
        ref, k = pieces[i]
        return copy(half_of(i, 1 - c), ref.at[k, own_block], core_sem.at[0, i], core_sem.at[1, i], partner)

    def share(i):
        local_copy(i).start()
        core_copy(i).start()

    def padded(array):
        rest = -array.shape[1] % 128
        return jnp.concatenate([array, jnp.zeros((array.shape[0], rest), array.dtype)], axis=1) if rest else array

    def head_part(array, cc, k, part):
        at = [((cc * na + k) * hp + h) * 3 * HEAD + part * HEAD for h in range(hp)]
        return padded(jnp.concatenate([array[:, a : a + HEAD] for a in at], axis=1))

    for cc in range(2):
        for k in range(na):
            for part in range(3):
                wa_in[cc, k, :, part * 128 : (part + 1) * 128] = head_part(w_qkv[...], cc, k, part)
            at = (cc * na + k) * wide
            wa_in[cc, k, :, 384:512] = padded(w_dense[:, at : at + wide])
    for i in A:
        share(i)
    for i in U + Dn:
        share(i)
    docs[c] = jnp.broadcast_to(segments[...].astype(F32), docs.shape[1:])
    docs_core = copy(
        docs.at[c], docs.at[c], core_sem.at[0, len(pieces)], core_sem.at[1, len(pieces)], partner
    )
    docs_core.start()

    def permute(rows):
        return jnp.concatenate(
            [rows[:, (zz * 2 + xx) * chip : (zz * 2 + xx + 1) * chip] for xx in range(2) for zz in range(nz)],
            axis=1,
        )

    def restore(rows):
        return jnp.concatenate(
            [rows[:, (xx * nz + zz) * chip : (xx * nz + zz + 1) * chip] for zz in range(nz) for xx in range(2)],
            axis=1,
        )

    def act_rows(cc, tt):
        return pl.ds(pl.multiple_of((cc * nt + tt) * R, R), R)

    tile = min(64, R)

    def norm_rows(j, carry):
        rows = pl.ds(pl.multiple_of(j * tile, tile), tile)
        normal, _ = normalize(tokens[rows, :].astype(F32))
        to = pl.ds(pl.multiple_of((c * nt + t) * R + j * tile, tile), tile)
        normed[to, :] = permute((normal * gain[...] + shift[...]).astype(BF16))
        grads[to, :] = permute(cotangent[rows, :])
        return carry

    lax.fori_loop(0, R // tile, norm_rows, 0)

    acts = (normed, grads)

    def prepare():
        for k in range(na):
            for part in range(3):
                ba[k, :, part * 128 : (part + 1) * 128] = jnp.where(
                    c == 0, head_part(b_qkv[...], 0, k, part), head_part(b_qkv[...], 1, k, part)
                )
        inverse = np.float32(ROTARY_BASE) ** (-(np.arange(ROT // 2, dtype=np.float32) * 2.0 / ROT)).astype(np.float32)
        lane = lax.broadcasted_iota(jnp.int32, (128, 128), 1) % HEAD
        scale = jnp.zeros((128, 128), F32)
        for j in range(ROT):
            scale = jnp.where(lane == j, inverse[j % (ROT // 2)], scale)

        def table(j, carry):
            rows = pl.ds(pl.multiple_of(j * 128, 128), 128)
            place = (j * 128 + lax.broadcasted_iota(jnp.int32, (128, 128), 0)).astype(F32)
            cos, sin = jnp.cos(place * scale), jnp.sin(place * scale)
            cos_table[rows, :] = cos
            sin_table[rows, :] = jnp.where(lane < ROT // 2, -sin, sin)
            return carry

        lax.fori_loop(0, length // 128, table, 0)

    def prepare_docs():
        docs_core.wait_recv()
        for j in range(length // 128):
            cut = slice(j * 128, (j + 1) * 128)
            both = [jnp.broadcast_to(docs[s, 0:1, cut], (HEAD, 128)) for s in range(2)]
            doc_column[cut, :] = jnp.transpose(jnp.concatenate(both, axis=0))

    def act_turn(a, tt, src_t):
        blk = acts[a].at[act_rows(c, src_t)]
        return copy(blk, blk, act_send.at[a, tt], act_recv.at[a, src_t], turned(tt))

    def act_core(a, src_t, cc):
        blk = acts[a].at[act_rows(cc, src_t)]
        return copy(blk, blk, pass_send.at[a, src_t], pass_recv.at[a, src_t], partner)

    for a in range(2):
        for k in range(1, nt):
            act_turn(a, other_t(k), t).start()
        act_core(a, t, c).start()

    def act_forward(a):
        for k in range(1, nt):
            src = other_t(k)
            act_turn(a, t, src).wait_recv()
            act_core(a, src, c).start()

    def act_sent(a):
        for k in range(nt):
            act_core(a, k, c).wait_send()
        for k in range(1, nt):
            act_turn(a, other_t(k), t).wait_send()

    def act_wait(a):
        for k in range(nt):
            act_core(a, k, 1 - c).wait_recv()

    def w_block(i, xx, zz):
        ref, k = pieces[i]
        return ref.at[k, chip_rows(xx, zz)]

    def send_up(i, src):
        b = w_block(i, x, src)
        return copy(b, b, up_send.at[i, src], z_recv.at[i, src], along(z + 1))

    def send_down(i, src):
        b = w_block(i, x, src)
        return copy(b, b, down_send.at[i, src], z_recv.at[i, src], along(z - 1))

    def send_across(i, src, xx):
        b = w_block(i, xx, src)
        return copy(b, b, x_send.at[i, src], x_recv.at[i, src], across)

    def send_own(i):
        local_copy(i).wait()
        core_copy(i).wait_recv()
        pl.when(z < nz - 1)(lambda: send_up(i, z).start())
        pl.when(z > 0)(lambda: send_down(i, z).start())
        send_across(i, z, x).start()

    def forward(i, d):
        @pl.when(z >= d)
        def _():
            send_up(i, z - d).wait_recv()
            pl.when(z < nz - 1)(lambda: send_up(i, z - d).start())
            send_across(i, z - d, x).start()

        @pl.when(z + d <= nz - 1)
        def _():
            send_down(i, z + d).wait_recv()
            pl.when(z > 0)(lambda: send_down(i, z + d).start())
            send_across(i, z + d, x).start()

    def gathered(i):
        for src in range(nz):
            send_across(i, src, 1 - x).wait_recv()

    def g_across(i, to_z):
        blk = pl.ds(to_z * chip, chip)
        return copy(xs_of[i].at[blk], xr_of[i].at[blk], rx_send.at[i, to_z], rx_recv.at[i, to_z], across)

    def g_along(i, to_z, src_z):
        blk = pl.ds(pl.multiple_of(to_z * chip, chip), chip)
        src = pl.ds(pl.multiple_of(src_z * chip, chip), chip)
        return copy(zs_of[i].at[blk], zr_of[i].at[src], rz_send.at[i, to_z], rz_recv.at[i, src_z], along(to_z))

    def g_final(i, cc):
        if i in A:
            dst = fr_a.at[i]
        elif i in U:
            dst = up_grad.at[:, pl.ds(pl.multiple_of(cc * units + (i - na) * pw, pw), pw)]
        else:
            dst = down_grad.at[:, pl.ds(pl.multiple_of(cc * units + (i - na - nm) * pw, pw), pw)]
        return copy(fs_of[i], dst, fin_send.at[i], fin_recv.at[i], partner)

    def columns(xx):
        return pl.ds(pl.multiple_of(xx * half, half), half)

    def products(i, xx):
        if i in A:
            k = i
            return [
                (0, 384, dot(normed[:, columns(xx)], grad_z[k], 0, 0)),
                (384, 512, dot(grads[:, columns(xx)], attended[k], 0, 0)),
            ]
        if i in U:
            k = i - na
            return [(0, pw, dot(normed[:, columns(xx)], grad_u[k], 0, 0))]
        k = i - na - nm
        return [(0, pw, dot(grads[:, columns(xx)], active[k], 0, 0))]

    def weight_grad(i):
        for lo, hi, part in products(i, 1 - x):
            xs_of[i][:, lo:hi] = part.astype(BF16)
        for to_z in range(nz):
            g_across(i, to_z).start()
        for lo, hi, part in products(i, x):
            own_of[i][:, lo:hi] = part

    def scatter_x(i):
        for to_z in range(nz):
            g_across(i, to_z).wait_recv()
            blk = slice(to_z * chip, (to_z + 1) * chip)
            both = own_of[i][blk, :] + xr_of[i][blk, :].astype(F32)

            @pl.when(to_z != z)
            def _():
                zs_of[i][blk, :] = both.astype(BF16)
                g_along(i, to_z, z).start()

            @pl.when(to_z == z)
            def _():
                own_of[i][blk, :] = both

    def scatter_z(i):
        total = own_of[i][pl.ds(pl.multiple_of(z * chip, chip), chip), :]
        for k in range(1, nz):
            src = other_z(k)
            g_along(i, z, src).wait_recv()
            total = total + zr_of[i][pl.ds(pl.multiple_of(src * chip, chip), chip), :].astype(F32)
        keep = jnp.where(c == 0, total[:r, :], total[r:, :])
        give = jnp.where(c == 0, total[r:, :], total[:r, :])
        if i in A:
            keep_a[i] = keep
        elif i in U:
            up_grad[:, pl.ds(pl.multiple_of(c * units + (i - na) * pw, pw), pw)] = keep
        else:
            down_grad[:, pl.ds(pl.multiple_of(c * units + (i - na - nm) * pw, pw), pw)] = keep
        fs_of[i][...] = give
        g_final(i, c).start()

    def finish_attention():
        for k in range(na):
            g_final(k, 1 - c).wait_recv()
            for cc in range(2):
                part = jnp.where(c == cc, keep_a[k], fr_a[k])
                heads = [
                    part[:, p * 128 + h * HEAD : p * 128 + (h + 1) * HEAD] for h in range(hp) for p in range(3)
                ]
                at = (cc * na + k) * wide
                qkv_grad[:, 3 * at : 3 * (at + wide)] = jnp.concatenate(heads, axis=1)
                dense_grad[:, at : at + wide] = part[:, 384 : 384 + wide]

    RT = min(512, 2 * length)
    tiles = 2 * length // RT
    lanes = lax.broadcasted_iota(jnp.int32, (1, 128), 1)
    first = lanes < HEAD

    low = lanes % HEAD < ROT // 2
    turning = lanes % HEAD < ROT

    def rotated(rows, places, sign):
        near = jnp.where(low, pltpu.roll(rows, 128 - ROT // 2, 1), pltpu.roll(rows, ROT // 2, 1))
        return rows * cos_table[places, :] + jnp.where(turning, sign * near * sin_table[places, :], 0.0)

    def project(k):
        def body(j, carry):
            rows = pl.ds(pl.multiple_of(j * RT, RT), RT)
            places = pl.ds(pl.multiple_of(lax.rem(j * RT, length), RT), RT)
            packed = dot(normed[rows, :], wa[k, :, 0:384], 1, 0) + ba[k]
            query[rows, :] = (rotated(packed[:, 0:128], places, 1.0) * (HEAD**-0.5)).astype(BF16)
            key[rows, :] = rotated(packed[:, 128:256], places, 1.0).astype(BF16)
            value[rows, :] = packed[:, 256:384].astype(BF16)
            grad_out[rows, :] = dot(grads[rows, :], wa[k, :, 384:512], 1, 0).astype(BF16)
            return carry

        lax.fori_loop(0, tiles, body, 0)

    block = min(128, length // 4)
    window = length // 4 + block

    def stacked(rows):
        if hp == 1:
            return rows
        zero = jnp.zeros_like(rows)
        return jnp.concatenate([jnp.where(first, rows, zero), jnp.where(first, zero, rows)], axis=0)

    def unstacked(rows):
        if hp == 1:
            return rows
        return jnp.where(first, rows[: window], rows[window :])

    def attend(k, s):
        key_sum[...] = jnp.zeros_like(key_sum)
        value_sum[...] = jnp.zeros_like(value_sum)

        def body(i, carry):
            q_at = pl.multiple_of(i * block, block)
            k_at = pl.multiple_of(jnp.maximum(q_at - length // 4, 0), block)
            q_rows = pl.ds(pl.multiple_of(s * length + q_at, block), block)
            k_rows = pl.ds(pl.multiple_of(s * length + k_at, block), window)
            q = query[q_rows, :]
            g = grad_out[q_rows, :]
            keys, values = stacked(key[k_rows, :]), stacked(value[k_rows, :])
            scores = dot(q, keys, 1, 1)
            grad_p = dot(g, values, 1, 1)
            at = k_at + lax.broadcasted_iota(jnp.int32, (block, window), 1)
            here = q_at + lax.broadcasted_iota(jnp.int32, (block, window), 0)
            allowed = (doc_column[pl.ds(q_at, block), s * HEAD : s * HEAD + 1] == docs[s, 0:1, pl.ds(k_at, window)]) & (at <= here)
            probs, grad_s = [], []
            for h in range(hp):
                cut = slice(h * window, (h + 1) * window)
                sc = jnp.where(allowed, scores[:, cut], -1e30)
                expos = jnp.exp(sc - jnp.max(sc, axis=-1, keepdims=True))
                p = expos / jnp.sum(expos, axis=-1, keepdims=True)
                gp = grad_p[:, cut]
                inner = jnp.sum(p * gp, axis=-1, keepdims=True)
                probs.append(p.astype(BF16))
                grad_s.append((p * (gp - inner)).astype(BF16))
            p = jnp.concatenate(probs, axis=1) if hp > 1 else probs[0]
            gs = jnp.concatenate(grad_s, axis=1) if hp > 1 else grad_s[0]
            attended[k, q_rows, :] = dot(p, values, 1, 0).astype(BF16)
            places = pl.ds(q_at, block)
            back = rotated(dot(gs, keys, 1, 0) * (HEAD**-0.5), places, -1.0)
            grad_z[k, q_rows, 0:128] = back.astype(BF16)
            here_rows = pl.ds(k_at, window)
            key_sum[here_rows, :] += unstacked(dot(gs, q, 0, 0))
            value_sum[here_rows, :] += unstacked(dot(p, g, 0, 0))
            return carry

        lax.fori_loop(0, length // block, body, 0)
        rows = pl.ds(pl.multiple_of(s * length, length), length)
        grad_z[k, rows, 128:256] = rotated(key_sum[...], slice(None), -1.0).astype(BF16)
        grad_z[k, rows, 256:384] = value_sum[...].astype(BF16)

    def hidden(k):
        def body(j, carry):
            rows = pl.ds(pl.multiple_of(j * RT, RT), RT)
            u = dot(normed[rows, :], wu[k], 1, 0) + b_up[:, pl.ds(pl.multiple_of(c * units + k * pw, pw), pw)]
            phi = 0.5 * (1.0 + lax.erf(u * np.float32(0.5**0.5)))
            active[k, rows, :] = (u * phi).astype(BF16)
            slope[k, rows, :] = phi + u * (jnp.exp(-0.5 * u * u) * np.float32((2 * np.pi) ** -0.5))
            return carry

        lax.fori_loop(0, tiles, body, 0)

    def hidden_back(k):
        def body(j, carry):
            rows = pl.ds(pl.multiple_of(j * RT, RT), RT)
            grad_u[k, rows, :] = (dot(grads[rows, :], wd[k], 1, 0) * slope[k, rows, :]).astype(BF16)
            return carry

        lax.fori_loop(0, tiles, body, 0)

    HT = min(512, length)

    def branch_rows(a, cc):
        def body(j, carry):
            rows = pl.ds(pl.multiple_of(cc * length + j * HT, HT), HT)
            total = None
            for k in range(na):
                if a == 0:
                    part = dot(attended[k, rows, :], wa[k, :, 384:512], 1, 1)
                else:
                    part = dot(grad_z[k, rows, :], wa[k, :, 0:384], 1, 1)
                total = part if total is None else total + part
            for k in range(nm):
                if a == 0:
                    part = dot(active[k, rows, :], wd[k], 1, 1)
                else:
                    part = dot(grad_u[k, rows, :], wu[k], 1, 1)
                total = total + part
            partials[a][rows, :] = total.astype(BF16)
            return carry

        lax.fori_loop(0, length // HT, body, 0)

    def half_copy(a, cc):
        rows = pl.ds(pl.multiple_of(cc * length, length), length)
        return copy(partials[a].at[rows], core_in, half_send.at[a], half_recv.at[a], partner)

    def branches(a):
        branch_rows(a, 1 - c)
        if a == 1:
            pl.semaphore_wait(credit.at[0], 1)
        half_copy(a, 1 - c).start()
        branch_rows(a, c)

    def turn_copy(a, tt, src):
        rows = pl.ds(pl.multiple_of(c * length + tt * R, R), R)
        return copy(
            partials[a].at[rows], turn_in.at[src], turn_send.at[a, tt], turn_recv.at[a, src], turned(tt)
        )

    def reduce_core(a):
        half_copy(a, 1 - c).wait()
        if a == 1 and nt > 1:
            pl.semaphore_wait(credit.at[1], nt - 1)
        for k in range(nt):
            tt = other_t(k)
            rows = pl.ds(pl.multiple_of(c * length + tt * R, R), R)
            mine = pl.ds(pl.multiple_of(tt * R, R), R)
            both = partials[a][rows, :].astype(F32) + core_in[mine, :].astype(F32)
            if k == 0:
                own_rows[...] = both
            else:
                partials[a][rows, :] = both.astype(BF16)
                turn_copy(a, tt, t).start()
        if a == 0:
            pl.semaphore_signal(credit.at[0], inc=1, device_id=partner, device_id_type=MESH)

    def reduced(a, rows):
        total = own_rows[rows, :]
        for k in range(1, nt):
            total = total + turn_in[other_t(k), rows, :].astype(F32)
        return restore(total)

    def reduce_turn(a):
        for k in range(1, nt):
            turn_copy(a, t, other_t(k)).wait_recv()

    def write_output():
        def body(j, carry):
            rows = pl.ds(pl.multiple_of(j * tile, tile), tile)
            total = tokens[rows, :].astype(F32) + reduced(0, rows) + b_dense[...] + b_down[...]
            output[rows, :] = total.astype(BF16)
            return carry

        lax.fori_loop(0, R // tile, body, 0)
        for k in range(1, nt):
            pl.semaphore_signal(credit.at[1], inc=1, device_id=turned(other_t(k)), device_id_type=MESH)

    def write_input_grad():
        vec[0] = jnp.zeros_like(vec[0])

        def body(j, carry):
            rows = pl.ds(pl.multiple_of(j * tile, tile), tile)
            normal, inverse = normalize(tokens[rows, :].astype(F32))
            up = cotangent[rows, :].astype(F32)
            grad = reduced(1, rows)
            vec[0, 0:1, :] += jnp.sum(grad * normal, axis=0, keepdims=True)
            vec[0, 1:2, :] += jnp.sum(grad, axis=0, keepdims=True)
            vec[0, 2:3, :] += jnp.sum(up, axis=0, keepdims=True)
            scaled = grad * gain[...]
            input_grad[rows, :] = up + inverse * (
                scaled
                - jnp.mean(scaled, axis=-1, keepdims=True)
                - normal * jnp.mean(scaled * normal, axis=-1, keepdims=True)
            )
            return carry

        lax.fori_loop(0, R // tile, body, 0)
        for k in range(nm):
            vec[0, 8:9, k * pw : (k + 1) * pw] = jnp.sum(grad_u[k].astype(F32), axis=0, keepdims=True)
        for k in range(na):
            vec[0, 9:10, k * 512 : k * 512 + 384] = jnp.sum(grad_z[k].astype(F32), axis=0, keepdims=True)

    top, bottom, whole = pl.ds(0, 8), pl.ds(8, 8), pl.ds(0, 16)

    def vec_copy(stage, rows, dst, slot, sem, to):
        return copy(
            vec.at[stage, rows], dst, vec_send.at[stage, slot], vec_recv.at[stage, sem], to
        )

    def small_sums():
        def add(first_sum, second_sum):
            return first_sum + second_sum

        core = vec_copy(0, top, vec_in.at[0, top], 0, 0, partner)
        core.start()
        core.wait_recv()
        vec[1, 0:8] = add(vec[0, 0:8], vec_in[0, 0:8])
        vec[1, 8:16] = vec[0, 8:16]
        vec_t[t] = vec[1, 0:8]
        for k in range(1, nt):
            vec_copy(1, top, vec_t.at[t], other_t(k), t, turned(other_t(k))).start()
        for k in range(1, nt):
            src = other_t(k)
            vec_copy(1, top, vec_t.at[src], t, src, turned(src)).wait_recv()
        total = vec_t[0]
        for k in range(1, nt):
            total = total + vec_t[k]
        vec[2, 0:8] = total
        vec[2, 8:16] = vec[1, 8:16]
        cross = vec_copy(2, whole, vec_in.at[1], 0, 0, across)
        cross.start()
        cross.wait_recv()
        vec[3] = add(vec[2], vec_in[1])
        vec_z[z] = vec[3]
        for k in range(1, nz):
            vec_copy(3, whole, vec_z.at[z], other_z(k), z, along(other_z(k))).start()
        for k in range(1, nz):
            src = other_z(k)
            vec_copy(3, whole, vec_z.at[src], z, src, along(src)).wait_recv()
        total = vec_z[0]
        for k in range(1, nz):
            total = total + vec_z[k]
        vec[4] = total
        last = vec_copy(4, bottom, vec_in.at[2, bottom], 0, 0, partner)
        last.start()
        gain_grad[...] = vec[4, 0:1]
        shift_grad[...] = vec[4, 1:2]
        dense_bias[...] = vec[4, 2:3]
        last.wait_recv()
        for cc in range(2):
            part = jnp.where(c == cc, vec[4, 8:10], vec_in[2, 8:10])
            up_bias[:, cc * units : (cc + 1) * units] = part[0:1, :units]
            for k in range(na):
                row = part[1:2, k * 512 : k * 512 + 384]
                heads = [row[:, p * 128 + h * HEAD : p * 128 + (h + 1) * HEAD] for h in range(hp) for p in range(3)]
                at = (cc * na + k) * wide
                qkv_bias[:, 3 * at : 3 * (at + wide)] = jnp.concatenate(heads, axis=1)
        core.wait_send()
        for k in range(1, nt):
            vec_copy(1, top, vec_t.at[t], other_t(k), t, turned(other_t(k))).wait_send()
        cross.wait_send()
        for k in range(1, nz):
            vec_copy(3, whole, vec_z.at[z], other_z(k), z, along(other_z(k))).wait_send()
        last.wait_send()

    steps = []

    def lead(i, n):
        for d in range(1, nz):
            for j in range(i, min(i + n, len(pieces))):
                steps.append(functools.partial(forward, j, d))
            if d == min(2, nz - 1):
                for j in range(i + n, min(i + 2 * n, len(pieces))):
                    steps.append(functools.partial(send_own, j))

    for i in range(0, len(pieces), 2):
        lead(i, 2)
    steps.reverse()

    def advance(n):
        for _ in range(n):
            if steps:
                steps.pop()()

    per = nz + 1
    send_own(0)
    if len(pieces) > 1:
        send_own(1)
    prepare()
    prepare_docs()
    advance(2)
    act_forward(0)
    advance(len(range(1, nz)) * 2 + 2 - 2)
    act_forward(1)
    act_wait(0)
    act_wait(1)
    for k in range(na):
        gathered(A[k])
        project(k)
        advance(per // 2)
        for s in range(2):
            attend(k, s)
            advance(per // 2)
        weight_grad(A[k])
        advance(1)
    for k in range(nm):
        if k == 0:
            advance(per * 2)
        gathered(U[k])
        hidden(k)
        advance(per)
        weight_grad(Dn[k])
        if k < na:
            scatter_x(A[k])
        advance(per)
    advance(len(steps))
    for k in range(na):
        if k >= nm:
            scatter_x(A[k])
        scatter_z(A[k])
    for k in range(nm):
        gathered(Dn[k])
        hidden_back(k)
        weight_grad(U[k])
        scatter_x(Dn[k])
    act_sent(1)
    act_sent(0)
    branches(0)
    reduce_core(0)
    branches(1)
    for k in range(nm):
        scatter_x(U[k])
    reduce_turn(0)
    write_output()
    reduce_core(1)
    for k in range(nm):
        scatter_z(Dn[k])
    reduce_turn(1)
    write_input_grad()
    small_sums()
    for k in range(nm):
        scatter_z(U[k])
    finish_attention()

    for i in range(len(pieces)):
        if i not in A:
            g_final(i, 1 - c).wait_recv()
        g_final(i, c).wait_send()
        core_copy(i).wait_send()
        for src in range(nz):
            pl.when((z < nz - 1) & (src <= z))(lambda: send_up(i, src).wait_send())
            pl.when((z > 0) & (src >= z))(lambda: send_down(i, src).wait_send())
            send_across(i, src, x).wait_send()
            g_across(i, src).wait_send()
            pl.when(src != z)(lambda: g_along(i, src, z).wait_send())
    for a in range(2):
        for k in range(1, nt):
            turn_copy(a, other_t(k), t).wait_send()
    docs_core.wait_send()


def on_device(
    nt,
    n_dp,
    tokens,
    cotangent,
    segments,
    ln_gain,
    ln_bias,
    w_qkv,
    b_qkv,
    w_dense,
    b_dense,
    w_up,
    b_up,
    w_down,
    b_down,
):
    R, D = tokens.shape
    length = segments.shape[1]
    r = w_qkv.shape[0]
    nz = n_dp // 4
    heads = w_qkv.shape[1] // (3 * HEAD) // 2
    hp = 2 if heads % 2 == 0 else 1
    na = heads // hp
    units = w_up.shape[1] // 2
    pw = 512 if units % 512 == 0 else units
    nm = units // pw
    wide = hp * HEAD
    sizes = dict(nt=nt, nz=nz, na=na, nm=nm, hp=hp, length=length, R=R, r=r, pw=pw)

    widths = ((na, 512), (nm, pw), (nm, pw))
    count = na + 2 * nm
    rows = 2 * length
    half = D // 2
    chip = 2 * r
    V = pltpu.VMEM
    DMA = pltpu.SemaphoreType.DMA
    scratch = (
        [V((2, na, r, 512), BF16), V((na, 1, 384), F32)]
        + [V((length, 128), F32)] * 2
        + [V((2, 8, length), F32), V((length, 128), F32)]
        + [V((n, D, w), BF16) for n, w in widths]
        + [V((rows, D), BF16), V((rows, D), BF16)]
        + [V((rows, 128), BF16)] * 4
        + [V((na, rows, 128), BF16), V((na, rows, 384), BF16)]
        + [V((length, 128), F32)] * 2
        + [V((nm, rows, pw), BF16), V((nm, rows, pw), F32), V((nm, rows, pw), BF16)]
        + [V((length, D), BF16), V((nt, R, D), BF16)]
        + [V((R, D), F32)]
        + [V((n, half, w), F32) for n, w in widths]
        + [V((n, half, w), BF16) for _ in range(4) for n, w in widths]
        + [V((na, r, 512), F32), V((nm, r, pw), F32), V((nm, r, pw), F32)]
        + [V((na, r, 512), F32)] * 2
        + [V((5, 16, D), F32), V((3, 16, D), F32), V((nt, 8, D), F32), V((nz, 16, D), F32)]
        + [DMA((count + 1,)), DMA((2, count + 1))]
        + [DMA((count, nz))] * 5
        + [DMA((2, nt))] * 4
        + [DMA((count, nz))] * 4
        + [DMA((count,))] * 2
        + [DMA((2,))] * 2
        + [DMA((2, nt))] * 2
        + [DMA((5, max(nt, nz)))] * 2
        + [pltpu.SemaphoreType.REGULAR((2,))]
    )
    space = pl.BlockSpec(memory_space=pltpu.VMEM)

    def row(vector):
        return vector.reshape(1, -1)

    args = (
        tokens,
        cotangent,
        segments,
        row(ln_gain),
        row(ln_bias),
        w_qkv,
        row(b_qkv),
        w_dense.T,
        row(b_dense),
        w_up,
        row(b_up),
        w_down.T,
        row(b_down),
    )
    shapes = (
        jax.ShapeDtypeStruct((R, D), BF16),
        jax.ShapeDtypeStruct((R, D), F32),
        jax.ShapeDtypeStruct((1, D), F32),
        jax.ShapeDtypeStruct((1, D), F32),
        jax.ShapeDtypeStruct(w_qkv.shape, F32),
        jax.ShapeDtypeStruct((1, w_qkv.shape[1]), F32),
        jax.ShapeDtypeStruct(w_dense.shape[::-1], F32),
        jax.ShapeDtypeStruct((1, D), F32),
        jax.ShapeDtypeStruct(w_up.shape, F32),
        jax.ShapeDtypeStruct((1, w_up.shape[1]), F32),
        jax.ShapeDtypeStruct(w_down.shape[::-1], F32),
    )
    out = pl.pallas_call(
        functools.partial(kernel, sizes),
        out_shape=shapes,
        in_specs=[space] * len(args),
        out_specs=[space] * len(shapes),
        scratch_shapes=scratch,
        compiler_params=pltpu.CompilerParams(
            collective_id=0, has_side_effects=True, vmem_limit_bytes=67043328
        ),
        name="layer",
    )(*args)
    out = [part.reshape(-1) if part.shape[0] == 1 else part for part in out]
    out[6], out[10] = out[6].T, out[10].T
    return (*out, out[7])


def solution(mesh):
    return jax.shard_map(
        functools.partial(on_device, mesh.shape["tensor"], mesh.shape["dp"]),
        mesh=mesh,
        in_specs=(
            P(("dp", "tensor"), None),
            P(("dp", "tensor"), None),
            P("dp", None),
            P(),
            P(),
            P("dp", "tensor"),
            P("tensor"),
            P("tensor", "dp"),
            P(),
            P("dp", "tensor"),
            P("tensor"),
            P("tensor", "dp"),
            P(),
        ),
        out_specs=(
            P(("dp", "tensor"), None),
            P(("dp", "tensor"), None),
            P(),
            P(),
            P("dp", "tensor"),
            P("tensor"),
            P("tensor", "dp"),
            P(),
            P("dp", "tensor"),
            P("tensor"),
            P("tensor", "dp"),
            P(),
        ),
        check_vma=False,
    )
```

profile of v0, /device:TPU:0, one launch (start us, length us, event | category | flops | bytes accessed | tf_op | source)
XLA Modules:
  0.0 193.3 jit_solution(5422948740346139522)
XLA Ops:
  0.6 1.3 reshape.59.b_qkv
  1.9 180.1 %layer.1 = (bf16[256,1024]{1,0:T(8,128)(2,1)}, f32[256,1024]{1,0:T(8,128)}, f32[1,1024]{1,0:T(1,128)}, f32[1,1024]{1,0:T(1,128)}, f32[64,1536]{1,0:T(8,128)}, /*...) custom-call(bf16[256,1024]{1,0:T(8,128)(2,1)} %tokens.1, ...), custom_call_target="tpu_custom_call" | custom-call | tf_op jit(solution)/shard_map/layer/pallas_call | solution.py:907
  182.0 0.0 copy-start
  182.0 1.4 reduce
  183.4 1.3 copy.36
  184.7 1.9 copy.37
  186.6 0.0 copy-done
  186.6 1.0 copy.38
  187.6 0.0 copy-done.8
  187.6 0.6 copy.39
  188.2 0.1 copy-done.7
  188.2 0.6 copy.40
  188.8 0.0 copy-done.3
  188.8 0.7 copy.41
  189.6 0.2 copy-done.4
  189.8 0.7 copy.42
  190.5 0.0 copy-done.5
  190.5 0.6 copy.43
  191.1 0.0 copy-done.2
  191.1 0.8 copy.44
  191.9 0.0 copy-done.6
  191.9 0.6 copy.45
  192.5 0.0 copy-done.1
  192.5 0.8 copy.46
  (8 shorter events, 0.0 us)
Async XLA Ops:
  182.0 4.5 %copy-start = (f32[256,1024]{1,0:T(8,128)S(1)}, f32[256,1024]{1,0:T(8,128)}, u32[]{:S(2)}) copy-start(f32[256,1024]{1,0:T(8,128)} %get-tuple-element.71) | copy-start | bytes 3145732
  186.6 1.0 copy-start.8
  186.6 2.3 %copy-start.3 = (f32[64,1536]{1,0:T(8,128)S(1)}, f32[64,1536]{1,0:T(8,128)}, u32[]{:S(2)}) copy-start(f32[64,1536]{1,0:T(8,128)} %get-tuple-element.74) | copy-start | bytes 1179652
  187.6 0.7 copy-start.7
  188.8 1.0 copy-start.4
  188.8 2.3 %copy-start.2 = (f32[64,2048]{1,0:T(8,128)S(1)}, f32[64,2048]{1,0:T(8,128)}, u32[]{:S(2)}) copy-start(f32[64,2048]{1,0:T(8,128)} %get-tuple-element.78) | copy-start | bytes 1572868
  189.8 0.7 copy-start.5
  191.1 0.8 copy-start.6
  191.1 1.4 copy-start.1
where the time goes:
time: 194 us; the launch traced here: 193 us
  Pallas kernels  180 us (93%)
  local copies, waits for them, and re-layouts  11.2 us (6%)
    pallas_call x1, Pallas kernels, on_device(): pl.pallas_call(functools.partial(kernel, sizes), out_shape=shapes, in_spe...  180 us
    unnamed x29, local copies, waits for them, and re-layouts  9.86 us

commit v1 on v0

v1 whole, which is shorter than its diff:
```python
import functools

import jax
import jax.numpy as jnp
import numpy as np
from jax import lax
from jax.experimental import pallas as pl
from jax.experimental.pallas import tpu as pltpu
from jax.sharding import PartitionSpec as P

HEAD = 64
ROT = 16
NORM_EPS = 1e-05
ROTARY_BASE = 10000.0
MESH = pl.DeviceIdType.MESH
F32 = jnp.float32
BF16 = jnp.bfloat16


def dot(left, right, over_left, over_right):
    return lax.dot_general(
        left, right, (((over_left,), (over_right,)), ((), ())), preferred_element_type=F32
    )


def normalize(rows):
    centred = rows - jnp.mean(rows, axis=-1, keepdims=True)
    inverse = lax.rsqrt(jnp.mean(centred * centred, axis=-1, keepdims=True) + NORM_EPS)
    return centred * inverse, inverse


def padded(array):
    rest = -array.shape[1] % 128
    return jnp.concatenate([array, jnp.zeros((array.shape[0], rest), array.dtype)], axis=1) if rest else array


def kernel(
    sizes,
    tokens,
    cotangent,
    segments,
    gain,
    shift,
    w_qkv,
    b_qkv,
    w_dense,
    b_dense,
    w_up,
    b_up,
    w_down,
    b_down,
    output,
    input_grad,
    gain_grad,
    shift_grad,
    qkv_grad,
    qkv_bias,
    dense_grad,
    dense_bias,
    up_grad,
    up_bias,
    down_grad,
    wa_in,
    ba,
    cos_table,
    sin_table,
    docs,
    doc_column,
    wa,
    wu,
    wd,
    normed,
    grads,
    query,
    key,
    value,
    grad_out,
    attended,
    grad_z,
    key_sum,
    value_sum,
    active,
    slope,
    grad_u,
    late,
    core_in,
    corner_x,
    corner_t,
    side_x,
    side_t,
    own_a,
    own_u,
    own_d,
    xs_a,
    xs_u,
    xs_d,
    xr_a,
    xr_u,
    xr_d,
    zs_a,
    zs_u,
    zs_d,
    zu_a,
    zu_u,
    zu_d,
    zd_a,
    zd_u,
    zd_d,
    fs_a,
    fs_u,
    fs_d,
    fr_a,
    fr_u,
    fr_d,
    vec,
    vec_z,
    vec_m,
    local_sem,
    share_send,
    share_recv,
    up_send,
    down_send,
    z_recv,
    x_send,
    x_recv,
    turn_send,
    turn_recv,
    side_send,
    side_recv,
    corner_x_send,
    corner_x_recv,
    corner_t_send,
    corner_t_recv,
    pass_send,
    pass_recv,
    gx_send,
    gx_recv,
    gu_send,
    gu_recv,
    gd_send,
    gd_recv,
    fin_send,
    fin_recv,
    half_send,
    half_recv,
    peer_send,
    peer_recv,
    mate_send,
    mate_recv,
    credit,
):
    nt, nz, gx, na, nm, hp, length, R, r, pw, nbuf = (
        sizes[k] for k in ("nt", "nz", "gx", "na", "nm", "hp", "length", "R", "r", "pw", "nbuf")
    )
    D = tokens.shape[1]
    chip = 2 * r
    zb = gx * chip
    own = D if gx == 2 else D // 2
    members = 2 * gx
    wide = hp * HEAD
    units = nm * pw
    total_rows = members * length
    partials = (grads, late if gx == 2 else normed)
    dp, t = lax.axis_index("dp"), lax.axis_index("tensor")
    z, x, c = dp // 4, (dp // 2) % 2, dp % 2
    j = c * gx + x if gx == 2 else c

    def device(zz, xx, cc, tt):
        return (zz * 4 + xx * 2 + cc, tt)

    partner = device(z, x, 1 - c, t)
    across = device(z, 1 - x, c, t)

    def member(jj):
        return device(z, jj % 2, jj // 2, t) if gx == 2 else device(z, x, jj, t)

    def along(zz):
        return device(zz, x, c, t)

    def turned(tt):
        return device(z, x, c, tt)

    def other_j(k):
        return lax.rem(j + k, members)

    def other_z(k):
        return lax.rem(z + k, nz)

    def other_t(k):
        return lax.rem(t + k, nt)

    def rows_at(start, size):
        return pl.ds(pl.multiple_of(start, size), size)

    def copy(src, dst, send, recv, to):
        return pltpu.make_async_remote_copy(
            src_ref=src, dst_ref=dst, send_sem=send, recv_sem=recv, device_id=to, device_id_type=MESH
        )

    A = list(range(na))
    U = list(range(na, na + nm))
    Dn = list(range(na + nm, na + 2 * nm))
    count = na + 2 * nm

    def of(a, u, d, i):
        if i in A:
            return a.at[i]
        return u.at[i - na] if i in U else d.at[i - na - nm]

    def weights(i):
        return of(wa, wu, wd, i)

    def z_rows(zz):
        return rows_at(zz * zb if gx == 2 else (x * nz + zz) * chip, zb)

    own_rows = rows_at(z * zb + (x * 2 + c) * r if gx == 2 else (x * nz + z) * chip + c * r, r)

    barrier = pltpu.get_barrier_semaphore()
    greeted = [member(other_j(k)) for k in range(1, members)] + ([] if gx == 2 else [across])
    if gx == 1:
        greeted += [device(other_z(k), 1 - x, c, t) for k in range(1, nz)]
    if nt > 1:
        greeted += [
            device(z, jj % 2 if gx == 2 else x, jj // 2 if gx == 2 else jj, other_t(k))
            for k in range(1, nt)
            for jj in [other_j(n) for n in range(1, members)]
        ]
    greeted += [along(other_z(k)) for k in range(1, nz)] + [turned(other_t(k)) for k in range(1, nt)]
    for other in greeted:
        pl.semaphore_signal(barrier, inc=1, device_id=other, device_id_type=MESH)

    def enter():
        pl.semaphore_wait(barrier, len(greeted))

    def part_of(i, jj):
        if i in A:
            return wa_in.at[jj, i]
        ref, k = (w_up, i - na) if i in U else (w_down, i - na - nm)
        return ref.at[:, rows_at(jj * units + k * pw, pw)]

    def local_copy(i):
        return pltpu.make_async_copy(part_of(i, j), weights(i).at[own_rows], local_sem.at[i])

    def give_part(i, jj):
        dst = weights(i).at[own_rows]
        return copy(part_of(i, jj), dst, share_send.at[i, jj], share_recv.at[i, j], member(jj))

    def take_part(i, jj):
        at = z * zb + (jj % 2 * 2 + jj // 2) * r if gx == 2 else (x * nz + z) * chip + jj * r
        dst = weights(i).at[rows_at(at, r)]
        return copy(part_of(i, j), dst, share_send.at[i, jj], share_recv.at[i, jj], member(jj))

    def share(i):
        local_copy(i).start()
        for k in range(1, members):
            give_part(i, other_j(k)).start()

    def head_part(array, jj, k, part):
        at = [((jj * na + k) * hp + h) * 3 * HEAD + part * HEAD for h in range(hp)]
        return padded(jnp.concatenate([array[:, a : a + HEAD] for a in at], axis=1))

    def own_doc(jj):
        return copy(docs.at[j], docs.at[j], share_send.at[count, jj], share_recv.at[count, j], member(jj))

    def doc_of(jj):
        return copy(docs.at[jj], docs.at[jj], share_send.at[count, jj], share_recv.at[count, jj], member(jj))

    def stage():
        for jj in range(members):
            for k in range(na):
                for part in range(3):
                    wa_in[jj, k, :, part * 128 : (part + 1) * 128] = head_part(w_qkv[...], jj, k, part)
                at = (jj * na + k) * wide
                wa_in[jj, k, :, 384:512] = padded(w_dense[:, at : at + wide])
        docs[j] = jnp.broadcast_to(segments[...].astype(F32), docs.shape[1:])

    def give_docs():
        for k in range(1, members):
            own_doc(other_j(k)).start()

    def permute(rows):
        if gx == 2:
            return rows
        return jnp.concatenate(
            [rows[:, (zz * 2 + xx) * chip : (zz * 2 + xx + 1) * chip] for xx in range(2) for zz in range(nz)],
            axis=1,
        )

    def restore(rows):
        if gx == 2:
            return rows
        return jnp.concatenate(
            [rows[:, (xx * nz + zz) * chip : (xx * nz + zz + 1) * chip] for zz in range(nz) for xx in range(2)],
            axis=1,
        )

    acts = (normed, grads)
    tile = min(64, R)
    split = D * 3 // 8
    left, right = slice(0, split), slice(split, D)

    def act_rows(jj, tt):
        return rows_at((jj * nt + tt) * R, R)

    across_j = c * gx + 1 - x if gx == 2 else c

    def fill_normed():
        def body(n, carry):
            rows = rows_at(n * tile, tile)
            normal, _ = normalize(tokens[rows, :].astype(F32))
            normed[rows_at((j * nt + t) * R + n * tile, tile), :] = permute(
                (normal * gain[...] + shift[...]).astype(BF16)
            )
            return carry

        lax.fori_loop(0, R // tile, body, 0)

    def fill_grads():
        def body(n, carry):
            grads[rows_at((j * nt + t) * R + n * tile, tile), :] = permute(cotangent[rows_at(n * tile, tile), :])
            return carry

        lax.fori_loop(0, R // tile, body, 0)

    def act_turn(a, tt, src):
        b = acts[a].at[act_rows(j, src)]
        return copy(b, b, turn_send.at[a, tt], turn_recv.at[a, src], turned(tt))

    def act_side(a, jj):
        b = acts[a].at[act_rows(jj, t)]
        return copy(b, b, side_send.at[a], side_recv.at[a], across)

    def act_corner_x(a, jj, tt):
        b = acts[a].at[act_rows(jj, tt), left]
        return copy(b, b, corner_x_send.at[a, tt], corner_x_recv.at[a, tt], across)

    def act_corner_t(a, tt, src):
        b = acts[a].at[act_rows(across_j, src), right]
        return copy(b, b, corner_t_send.at[a, tt], corner_t_recv.at[a, src], turned(tt))

    def act_pass(a, jj, tt):
        b = acts[a].at[act_rows(jj, tt)]
        return copy(b, b, pass_send.at[a, jj, tt], pass_recv.at[a, jj, tt], partner)

    def act_start(a):
        if gx == 2:
            act_side(a, j).start()
        for k in range(1, nt):
            act_turn(a, other_t(k), t).start()
        act_pass(a, j, t).start()

    def act_from_turn(a):
        for k in range(1, nt):
            src = other_t(k)
            act_turn(a, t, src).wait_recv()
            if gx == 2:
                act_corner_x(a, j, src).start()
            act_pass(a, j, src).start()

    def act_from_side(a):
        if gx == 2:
            act_side(a, across_j).wait_recv()
            for k in range(1, nt):
                act_corner_t(a, other_t(k), t).start()
            act_pass(a, across_j, t).start()

    def act_finish(a):
        if gx == 2:
            for k in range(1, nt):
                src = other_t(k)
                act_corner_x(a, across_j, src).wait_recv()
                act_corner_t(a, t, src).wait_recv()
                act_pass(a, across_j, src).start()

    def act_wait(a):
        for xx in range(gx):
            for k in range(nt):
                act_pass(a, (1 - c) * gx + xx, k).wait_recv()

    def act_sent(a):
        if gx == 2:
            act_side(a, j).wait_send()
        for k in range(1, nt):
            act_turn(a, other_t(k), t).wait_send()
            if gx == 2:
                act_corner_x(a, j, other_t(k)).wait_send()
                act_corner_t(a, other_t(k), t).wait_send()
        for xx in range(gx):
            for k in range(nt):
                act_pass(a, c * gx + xx, k).wait_send()

    def w_block(i, zz):
        return weights(i).at[z_rows(zz)]

    def send_up(i, src):
        b = w_block(i, src)
        return copy(b, b, up_send.at[i, src], z_recv.at[i, src], along(z + 1))

    def send_down(i, src):
        b = w_block(i, src)
        return copy(b, b, down_send.at[i, src], z_recv.at[i, src], along(z - 1))

    def send_across(i, src, xx):
        b = weights(i).at[rows_at((xx * nz + src) * chip, chip)]
        return copy(b, b, x_send.at[i, src], x_recv.at[i, src], across)

    def send_own(i):
        local_copy(i).wait()
        for k in range(1, members):
            take_part(i, other_j(k)).wait_recv()
        pl.when(z < nz - 1)(lambda: send_up(i, z).start())
        pl.when(z > 0)(lambda: send_down(i, z).start())
        if gx == 1:
            send_across(i, z, x).start()

    def forward_up(i, d):
        @pl.when(z >= d)
        def _():
            send_up(i, z - d).wait_recv()
            pl.when(z < nz - 1)(lambda: send_up(i, z - d).start())
            if gx == 1:
                send_across(i, z - d, x).start()

    def forward_down(i, d):
        @pl.when(z + d <= nz - 1)
        def _():
            send_down(i, z + d).wait_recv()
            pl.when(z > 0)(lambda: send_down(i, z + d).start())
            if gx == 1:
                send_across(i, z + d, x).start()

    def gathered(i):
        if gx == 1:
            for src in range(nz):
                send_across(i, src, 1 - x).wait_recv()

    def own_of(i):
        return of(own_a, own_u, own_d, i)

    def g_across(i, to_z):
        b = pl.ds(to_z * chip, chip)
        return copy(
            of(xs_a, xs_u, xs_d, i).at[b],
            of(xr_a, xr_u, xr_d, i).at[b],
            gx_send.at[i, to_z],
            gx_recv.at[i, to_z],
            across,
        )

    def g_up(i, to_z):
        b = rows_at(to_z * zb, zb)
        return copy(
            of(zs_a, zs_u, zs_d, i).at[b],
            of(zu_a, zu_u, zu_d, i).at[b],
            gu_send.at[i, to_z],
            gu_recv.at[i, to_z],
            along(z + 1),
        )

    def g_down(i, to_z):
        b = rows_at(to_z * zb, zb)
        return copy(
            of(zs_a, zs_u, zs_d, i).at[b],
            of(zd_a, zd_u, zd_d, i).at[b],
            gd_send.at[i, to_z],
            gd_recv.at[i, to_z],
            along(z - 1),
        )

    def g_final(i, jj, src):
        at = (jj % 2 * 2 + jj // 2) * r if gx == 2 else jj * r
        return copy(
            of(fs_a, fs_u, fs_d, i).at[rows_at(at, r)],
            of(fr_a, fr_u, fr_d, i).at[src],
            fin_send.at[i, jj],
            fin_recv.at[i, src],
            member(jj),
        )

    def products(i, columns):
        if i in A:
            return [
                (0, 384, dot(normed[:, columns], grad_z[i], 0, 0)),
                (384, 512, dot(grads[:, columns], attended[i], 0, 0)),
            ]
        if i in U:
            return [(0, pw, dot(normed[:, columns], grad_u[i - na], 0, 0))]
        return [(0, pw, dot(grads[:, columns], active[i - na - nm], 0, 0))]

    def weight_grad(i):
        cut = min(512, own)
        if gx == 1:
            xs = of(xs_a, xs_u, xs_d, i)
            for n in range(own // cut):
                for lo, hi, part in products(i, rows_at((1 - x) * own + n * cut, cut)):
                    xs[n * cut : (n + 1) * cut, lo:hi] = part.astype(BF16)
            for to_z in range(nz):
                g_across(i, to_z).start()
        for n in range(own // cut):
            at = n * cut if gx == 2 else x * own + n * cut
            for lo, hi, part in products(i, rows_at(at, cut)):
                own_of(i)[n * cut : (n + 1) * cut, lo:hi] = part

    def sum_x(i):
        if gx == 1:
            xr = of(xr_a, xr_u, xr_d, i)
            for to_z in range(nz):
                g_across(i, to_z).wait_recv()
                b = slice(to_z * chip, (to_z + 1) * chip)
                own_of(i)[b, :] += xr[b, :].astype(F32)

    def chain_step(i, to_z, last, came, buffer, send):
        b = rows_at(to_z * zb, zb)
        zs = of(zs_a, zs_u, zs_d, i)

        @pl.when(last)
        def _():
            zs[b, :] = own_of(i)[b, :].astype(BF16)

        @pl.when(jnp.logical_not(last))
        def _():
            came.wait_recv()
            zs[b, :] = (own_of(i)[b, :] + buffer[b, :].astype(F32)).astype(BF16)

        send.start()

    def chain_up(i, n):
        @pl.when(z <= n)
        def _():
            to_z = nz - 1 - n + z
            chain_step(i, to_z, z == 0, g_up(i, to_z), of(zu_a, zu_u, zu_d, i), g_up(i, to_z))

    def chain_down(i, n):
        @pl.when(nz - 1 - z <= n)
        def _():
            to_z = n - (nz - 1 - z)
            chain_step(i, to_z, z == nz - 1, g_down(i, to_z), of(zd_a, zd_u, zd_d, i), g_down(i, to_z))

    def own_index():
        return x * 2 + c if gx == 2 else c

    def chain_end(i):
        b = rows_at(z * zb, zb)

        @pl.when(z > 0)
        def _():
            g_up(i, z).wait_recv()
            own_of(i)[b, :] += of(zu_a, zu_u, zu_d, i)[b, :].astype(F32)

        @pl.when(z < nz - 1)
        def _():
            g_down(i, z).wait_recv()
            own_of(i)[b, :] += of(zd_a, zd_u, zd_d, i)[b, :].astype(F32)

        of(fs_a, fs_u, fs_d, i)[...] = own_of(i)[b, :].astype(BF16)
        for k in range(1, members):
            g_final(i, other_j(k), j).start()

    def finish(i):
        for k in range(1, members):
            g_final(i, j, other_j(k)).wait_recv()
        keep = own_of(i)[rows_at(z * zb + own_index() * r, r), :]
        came = of(fr_a, fr_u, fr_d, i)
        for jj in range(members):
            part = jnp.where(j == jj, keep, came[jj].astype(F32))
            if i in A:
                heads = [
                    part[:, p * 128 + h * HEAD : p * 128 + (h + 1) * HEAD] for h in range(hp) for p in range(3)
                ]
                at = (jj * na + i) * wide
                qkv_grad[:, 3 * at : 3 * (at + wide)] = jnp.concatenate(heads, axis=1)
                dense_grad[:, at : at + wide] = part[:, 384 : 384 + wide]
            else:
                out, k = (up_grad, i - na) if i in U else (down_grad, i - na - nm)
                out[:, jj * units + k * pw : jj * units + (k + 1) * pw] = part

    def pick(parts):
        total = parts[0]
        for jj in range(1, members):
            total = jnp.where(j == jj, parts[jj], total)
        return total

    def prepare():
        for k in range(na):
            for part in range(3):
                ba[k, :, part * 128 : (part + 1) * 128] = pick(
                    [head_part(b_qkv[...], jj, k, part) for jj in range(members)]
                )
        steps = np.arange(ROT // 2, dtype=np.float32) * 2.0 / ROT
        inverse = (np.float32(ROTARY_BASE) ** -steps).astype(np.float32)
        lane = lax.broadcasted_iota(jnp.int32, (128, 128), 1) % HEAD
        scale = jnp.zeros((128, 128), F32)
        for n in range(ROT):
            scale = jnp.where(lane == n, inverse[n % (ROT // 2)], scale)

        def table(n, carry):
            rows = rows_at(n * 128, 128)
            place = (n * 128 + lax.broadcasted_iota(jnp.int32, (128, 128), 0)).astype(F32)
            cos, sin = jnp.cos(place * scale), jnp.sin(place * scale)
            cos_table[rows, :] = cos
            sin_table[rows, :] = jnp.where(lane < ROT // 2, -sin, sin)
            return carry

        lax.fori_loop(0, length // 128, table, 0)

    lanes_of_doc = 128 // members

    def prepare_docs():
        for k in range(1, members):
            doc_of(other_j(k)).wait_recv()
        for n in range(length // 128):
            cut = slice(n * 128, (n + 1) * 128)
            rows = [jnp.broadcast_to(docs[s, 0:1, cut], (lanes_of_doc, 128)) for s in range(members)]
            doc_column[cut, :] = jnp.transpose(jnp.concatenate(rows, axis=0))

    RT = min(512, total_rows)
    tiles = total_rows // RT
    lanes = lax.broadcasted_iota(jnp.int32, (1, 128), 1)
    first = lanes < HEAD
    low = lanes % HEAD < ROT // 2
    turning = lanes % HEAD < ROT

    def rotated(rows, places, sign):
        near = jnp.where(low, pltpu.roll(rows, 128 - ROT // 2, 1), pltpu.roll(rows, ROT // 2, 1))
        return rows * cos_table[places, :] + jnp.where(turning, sign * near * sin_table[places, :], 0.0)

    def project(k, n):
        rows = rows_at(n * RT, RT)
        places = rows_at(lax.rem(n * RT, length), RT)
        packed = dot(normed[rows, :], wa[k, :, 0:384], 1, 0) + ba[k]
        query[rows, :] = (rotated(packed[:, 0:128], places, 1.0) * (HEAD**-0.5)).astype(BF16)
        key[rows, :] = rotated(packed[:, 128:256], places, 1.0).astype(BF16)
        value[rows, :] = packed[:, 256:384].astype(BF16)

    def project_back(k, n):
        rows = rows_at(n * RT, RT)
        grad_out[rows, :] = dot(grads[rows, :], wa[k, :, 384:512], 1, 0).astype(BF16)

    def each_tile(step, k):
        def body(n, carry):
            step(k, n)
            return carry

        lax.fori_loop(0, tiles, body, 0)

    block = min(128, length // 4)
    window = length // 4 + block

    def stacked(rows):
        if hp == 1:
            return rows
        zero = jnp.zeros_like(rows)
        return jnp.concatenate([jnp.where(first, rows, zero), jnp.where(first, zero, rows)], axis=0)

    def unstacked(rows):
        if hp == 1:
            return rows
        return jnp.where(first, rows[:window], rows[window:])

    def attend(k, s):
        key_sum[...] = jnp.zeros_like(key_sum)
        value_sum[...] = jnp.zeros_like(value_sum)

        def body(n, carry):
            q_at = pl.multiple_of(n * block, block)
            k_at = pl.multiple_of(jnp.maximum(q_at - length // 4, 0), block)
            q_rows = rows_at(s * length + q_at, block)
            k_rows = pl.ds(pl.multiple_of(s * length + k_at, block), window)
            q = query[q_rows, :]
            g = grad_out[q_rows, :]
            keys, values = stacked(key[k_rows, :]), stacked(value[k_rows, :])
            scores = dot(q, keys, 1, 1)
            grad_p = dot(g, values, 1, 1)
            at = k_at + lax.broadcasted_iota(jnp.int32, (block, window), 1)
            here = q_at + lax.broadcasted_iota(jnp.int32, (block, window), 0)
            lane = s * lanes_of_doc
            same = doc_column[pl.ds(q_at, block), lane : lane + 1] == docs[s, 0:1, pl.ds(k_at, window)]
            allowed = same & (at <= here)
            probs, grad_s = [], []
            for h in range(hp):
                cut = slice(h * window, (h + 1) * window)
                sc = jnp.where(allowed, scores[:, cut], -1e30)
                expos = jnp.exp(sc - jnp.max(sc, axis=-1, keepdims=True))
                p = expos / jnp.sum(expos, axis=-1, keepdims=True)
                gp = grad_p[:, cut]
                inner = jnp.sum(p * gp, axis=-1, keepdims=True)
                probs.append(p.astype(BF16))
                grad_s.append((p * (gp - inner)).astype(BF16))
            p = jnp.concatenate(probs, axis=1) if hp > 1 else probs[0]
            gs = jnp.concatenate(grad_s, axis=1) if hp > 1 else grad_s[0]
            attended[k, q_rows, :] = dot(p, values, 1, 0).astype(BF16)
            places = pl.ds(q_at, block)
            back = rotated(dot(gs, keys, 1, 0) * (HEAD**-0.5), places, -1.0)
            grad_z[k, q_rows, 0:128] = back.astype(BF16)
            here_rows = pl.ds(k_at, window)
            key_sum[here_rows, :] += unstacked(dot(gs, q, 0, 0))
            value_sum[here_rows, :] += unstacked(dot(p, g, 0, 0))
            return carry

        lax.fori_loop(0, length // block, body, 0)
        rows = rows_at(s * length, length)
        grad_z[k, rows, 128:256] = rotated(key_sum[...], slice(None), -1.0).astype(BF16)
        grad_z[k, rows, 256:384] = value_sum[...].astype(BF16)

    def hidden(k, n):
        rows = rows_at(n * RT, RT)
        u = dot(normed[rows, :], wu[k], 1, 0) + b_up[:, rows_at(j * units + k * pw, pw)]
        phi = 0.5 * (1.0 + lax.erf(u * np.float32(0.5**0.5)))
        active[k, rows, :] = (u * phi).astype(BF16)
        slope[k, rows, :] = phi + u * (jnp.exp(-0.5 * u * u) * np.float32((2 * np.pi) ** -0.5))

    def hidden_back(k, n):
        rows = rows_at(n * RT, RT)
        grad_u[k, rows, :] = (dot(grads[rows, :], wd[k], 1, 0) * slope[k, rows, :]).astype(BF16)

    per_core = gx * length
    HT = min(512, per_core)

    def branch_rows(a, cc):
        def body(n, carry):
            rows = rows_at(cc * per_core + n * HT, HT)
            total = None
            for k in range(na):
                if a == 0:
                    part = dot(attended[k, rows, :], wa[k, :, 384:512], 1, 1)
                else:
                    part = dot(grad_z[k, rows, :], wa[k, :, 0:384], 1, 1)
                total = part if total is None else total + part
            for k in range(nm):
                if a == 0:
                    part = dot(active[k, rows, :], wd[k], 1, 1)
                else:
                    part = dot(grad_u[k, rows, :], wu[k], 1, 1)
                total = total + part
            partials[a][rows, :] = total.astype(BF16)
            return carry

        lax.fori_loop(0, per_core // HT, body, 0)

    def half_copy(a, cc):
        rows = rows_at(cc * per_core, per_core)
        return copy(partials[a].at[rows], core_in.at[a % nbuf], half_send.at[a], half_recv.at[a], partner)

    def branches_give(a):
        branch_rows(a, 1 - c)
        if nbuf == 1 and a == second:
            pl.semaphore_wait(credit.at[0], 1)
        half_copy(a, 1 - c).start()

    def branches_keep(a):
        branch_rows(a, c)

    def block_rows(jj, tt):
        return rows_at((jj * nt + tt) * R, R)

    def in_rows(jj, tt):
        return rows_at(((jj - c * gx) * nt + tt) * R, R)

    def both_cores(a, jj, tt, columns=slice(None)):
        return (
            partials[a][block_rows(jj, tt), columns].astype(F32)
            + core_in[a % nbuf, in_rows(jj, tt), columns].astype(F32)
        )

    def corner_t_copy(a, tt, src):
        b = partials[a].at[block_rows(across_j, tt), left]
        return copy(b, corner_t.at[a % nbuf, src], corner_t_send.at[2 + a, tt], corner_t_recv.at[2 + a, src], turned(tt))

    def corner_x_copy(a, jj, tt):
        b = partials[a].at[block_rows(jj, tt), right]
        return copy(b, corner_x.at[a % nbuf, tt], corner_x_send.at[2 + a, tt], corner_x_recv.at[2 + a, tt], across)

    def side_copy(a, jj):
        b = partials[a].at[block_rows(jj, t)]
        return copy(b, side_x.at[a % nbuf], side_send.at[2 + a], side_recv.at[2 + a], across)

    def turn_copy(a, tt, src):
        b = partials[a].at[block_rows(j, tt)]
        return copy(b, side_t.at[a % nbuf, src], turn_send.at[2 + a, tt], turn_recv.at[2 + a, src], turned(tt))

    def reduce_corner(a):
        half_copy(a, 1 - c).wait_recv()
        if gx == 2:
            for k in range(1, nt):
                tt = other_t(k)
                partials[a][block_rows(across_j, tt), :] = both_cores(a, across_j, tt).astype(BF16)
                corner_t_copy(a, tt, t).start()
                corner_x_copy(a, across_j, tt).start()

    def reduce_side(a):
        if gx == 2:
            total = both_cores(a, across_j, t, left)
            for k in range(1, nt):
                corner_t_copy(a, t, other_t(k)).wait_recv()
                total = total + corner_t[a % nbuf, other_t(k)].astype(F32)
            partials[a][block_rows(across_j, t), left] = total.astype(BF16)
            partials[a][block_rows(across_j, t), right] = both_cores(a, across_j, t, right).astype(BF16)
            side_copy(a, across_j).start()

    def reduce_turn(a):
        if nbuf == 1 and a == second and nt > 1:
            pl.semaphore_wait(credit.at[1], nt - 1)
        for k in range(1, nt):
            tt = other_t(k)
            if gx == 2:
                corner_x_copy(a, j, tt).wait_recv()
                total = both_cores(a, j, tt, right) + corner_x[a % nbuf, tt].astype(F32)
                partials[a][block_rows(j, tt), right] = total.astype(BF16)
                partials[a][block_rows(j, tt), left] = both_cores(a, j, tt, left).astype(BF16)
            else:
                partials[a][block_rows(j, tt), :] = both_cores(a, j, tt).astype(BF16)
            turn_copy(a, tt, t).start()

    def reduce_wait(a):
        if gx == 2:
            side_copy(a, across_j).wait_recv()
        for k in range(1, nt):
            turn_copy(a, t, other_t(k)).wait_recv()

    def reduced(a, n):
        mine = rows_at((j * nt + t) * R + n * tile, tile)
        came = rows_at(((j - c * gx) * nt + t) * R + n * tile, tile)
        rows = rows_at(n * tile, tile)
        total = partials[a][mine, :].astype(F32) + core_in[a % nbuf, came, :].astype(F32)
        if gx == 2:
            total = total + side_x[a % nbuf, rows, :].astype(F32)
        for k in range(1, nt):
            total = total + side_t[a % nbuf, other_t(k), rows, :].astype(F32)
        return restore(total)

    def reduce_sent(a):
        half_copy(a, 1 - c).wait_send()
        if gx == 2:
            side_copy(a, across_j).wait_send()
        for k in range(1, nt):
            tt = other_t(k)
            turn_copy(a, tt, t).wait_send()
            if gx == 2:
                corner_t_copy(a, tt, t).wait_send()
                corner_x_copy(a, across_j, tt).wait_send()

    def free_buffers():
        if nbuf == 1:
            pl.semaphore_signal(credit.at[0], inc=1, device_id=partner, device_id_type=MESH)
            for k in range(1, nt):
                pl.semaphore_signal(credit.at[1], inc=1, device_id=turned(other_t(k)), device_id_type=MESH)

    def write_output():
        def body(n, carry):
            rows = rows_at(n * tile, tile)
            total = tokens[rows, :].astype(F32) + reduced(0, n) + b_dense[...] + b_down[...]
            output[rows, :] = total.astype(BF16)
            return carry

        lax.fori_loop(0, R // tile, body, 0)

    def sum_biases():
        vec[...] = jnp.zeros_like(vec)
        for k in range(nm):
            vec[3:4, k * pw : (k + 1) * pw] = jnp.sum(grad_u[k].astype(F32), axis=0, keepdims=True)
        for k in range(na):
            at = units + k * 384
            vec[3:4, at : at + 384] = jnp.sum(grad_z[k].astype(F32), axis=0, keepdims=True)

    def write_input_grad():
        def body(n, carry):
            rows = rows_at(n * tile, tile)
            normal, inverse = normalize(tokens[rows, :].astype(F32))
            up = cotangent[rows, :].astype(F32)
            grad = reduced(1, n)
            vec[0:1, :] += jnp.sum(grad * normal, axis=0, keepdims=True)
            vec[1:2, :] += jnp.sum(grad, axis=0, keepdims=True)
            vec[2:3, :] += jnp.sum(up, axis=0, keepdims=True)
            scaled = grad * gain[...]
            input_grad[rows, :] = up + inverse * (
                scaled
                - jnp.mean(scaled, axis=-1, keepdims=True)
                - normal * jnp.mean(scaled * normal, axis=-1, keepdims=True)
            )
            return carry

        lax.fori_loop(0, R // tile, body, 0)

    peers = nz if gx == 2 else 2 * nz
    mates = members * nt
    peer = z if gx == 2 else z * 2 + x
    mate = j * nt + t

    def peer_copy(to, src):
        device_to = device(to, x, c, t) if gx == 2 else device(to // 2, to % 2, c, t)
        return copy(vec_z.at[peer], vec_z.at[src], peer_send.at[to], peer_recv.at[src], device_to)

    def mate_copy(to, src):
        jj, tt = to // nt, to % nt
        device_to = device(z, jj % 2, jj // 2, tt) if gx == 2 else device(z, x, jj, tt)
        return copy(vec_m.at[mate], vec_m.at[src], mate_send.at[to], mate_recv.at[src], device_to)

    def sums_start():
        vec_z[peer] = vec[...]
        for k in range(1, peers):
            peer_copy(lax.rem(peer + k, peers), peer).start()

    def sums_group():
        for k in range(1, peers):
            peer_copy(peer, lax.rem(peer + k, peers)).wait_recv()
        total = vec_z[0]
        for k in range(1, peers):
            total = total + vec_z[k]
        vec_m[mate] = total
        for k in range(1, mates):
            mate_copy(lax.rem(mate + k, mates), mate).start()

    def sums_end():
        for k in range(1, mates):
            mate_copy(mate, lax.rem(mate + k, mates)).wait_recv()
        total = vec_m[0]
        for k in range(1, mates):
            total = total + vec_m[k]
        gain_grad[...] = total[0:1]
        shift_grad[...] = total[1:2]
        dense_bias[...] = total[2:3]
        for jj in range(members):
            row = vec_m[jj * nt + t][3:4]
            up_bias[:, jj * units : (jj + 1) * units] = row[:, :units]
            for k in range(na):
                part = row[:, units + k * 384 : units + (k + 1) * 384]
                heads = [part[:, p * 128 + h * HEAD : p * 128 + (h + 1) * HEAD] for h in range(hp) for p in range(3)]
                at = (jj * na + k) * wide
                qkv_bias[:, 3 * at : 3 * (at + wide)] = jnp.concatenate(heads, axis=1)

    def sums_sent():
        for k in range(1, peers):
            peer_copy(lax.rem(peer + k, peers), peer).wait_send()
        for k in range(1, mates):
            mate_copy(lax.rem(mate + k, mates), mate).wait_send()

    def forwards(some, lo, hi):
        for d in range(lo, hi):
            for i in some:
                forward_up(i, d)
                forward_down(i, d)

    def chains(some, lo, hi):
        for n in range(lo, hi):
            for i in some:
                chain_up(i, n)
                chain_down(i, n)

    second = 0 if gx == 2 else 1

    def any_order():
        stage()
        fill_normed()
        enter()
        for i in U + A + Dn:
            share(i)
        give_docs()
        act_start(0)
        fill_grads()
        act_start(1)
        for i in U + A:
            send_own(i)
        prepare()
        prepare_docs()
        forwards(U + A, 1, 2)
        act_from_turn(0)
        act_from_side(0)
        for i in Dn:
            send_own(i)
        forwards(U, 2, nz)
        act_finish(0)
        act_wait(0)
        for i in U:
            gathered(i)
            each_tile(hidden, i - na)
        act_from_turn(1)
        act_from_side(1)
        forwards(A, 2, nz)
        forwards(Dn, 1, nz)
        act_finish(1)
        act_wait(1)
        for i in Dn:
            weight_grad(i)
            sum_x(i)
        chains(Dn, 0, nz - 1)
        for i in A:
            gathered(i)
            each_tile(project, i)
            each_tile(project_back, i)
            for s in range(members):
                attend(i, s)
            weight_grad(i)
            sum_x(i)
        chains(A, 0, nz - 1)
        for i in Dn:
            gathered(i)
            each_tile(hidden_back, i - na - nm)
        for i in U:
            weight_grad(i)
            sum_x(i)
        act_sent(0)
        act_sent(1)
        sum_biases()
        for a in (1, 0) if gx == 2 else (0, 1):
            branches_give(a)
            branches_keep(a)
            reduce_corner(a)
            if a != second:
                chains(U, 0, nz - 1)
            reduce_side(a)
            reduce_turn(a)
            if a != second:
                for i in Dn + A:
                    chain_end(i)
            reduce_wait(a)
            if a == 0:
                write_output()
            else:
                write_input_grad()
                sums_start()
            if a != second:
                free_buffers()
        for i in U:
            chain_end(i)
        sums_group()
        for i in Dn + A + U:
            finish(i)
        sums_end()

    def tuned_order():
        (a,), (u,), (d,) = A, U, Dn
        fill_normed()
        stage()
        enter()
        share(u)
        share(a)
        give_docs()
        fill_grads()
        send_own(u)
        act_start(0)
        send_own(a)
        forward_up(u, 1)
        forward_down(u, 1)
        act_start(1)
        act_from_side(0)
        forward_down(a, 1)
        act_from_turn(0)
        forward_up(a, 1)
        share(d)
        forward_down(u, 2)
        forward_down(a, 2)
        forward_up(u, 2)
        act_from_side(1)
        act_from_turn(1)
        forward_up(a, 2)
        prepare_docs()
        act_finish(0)
        forward_up(u, 3)
        act_wait(0)
        forward_down(u, 3)
        hidden(0, 1)
        prepare()
        send_own(d)
        hidden(0, 2)
        forward_down(a, 3)
        forward_up(a, 3)
        project(0, 0)
        hidden(0, 3)
        project(0, 2)
        project(0, 3)
        hidden(0, 0)
        act_finish(1)
        project(0, 1)
        act_wait(1)
        weight_grad(d)
        chain_up(d, 0)
        chain_down(d, 0)
        forward_up(d, 1)
        forward_down(d, 1)
        each_tile(project_back, 0)
        attend(0, 0)
        attend(0, 1)
        forward_up(d, 2)
        chain_down(d, 1)
        forward_down(d, 2)
        chain_up(d, 1)
        attend(0, 3)
        attend(0, 2)
        weight_grad(a)
        forward_down(d, 3)
        forward_up(d, 3)
        chain_down(d, 2)
        chain_up(d, 2)
        hidden_back(0, 2)
        hidden_back(0, 0)
        hidden_back(0, 3)
        hidden_back(0, 1)
        weight_grad(u)
        chain_up(a, 0)
        branches_give(1)
        chain_down(a, 0)
        act_sent(0)
        act_sent(1)
        branches_give(0)
        chain_end(d)
        branches_keep(1)
        reduce_corner(1)
        chain_down(u, 0)
        branches_keep(0)
        chain_up(u, 0)
        reduce_corner(0)
        finish(d)
        reduce_side(1)
        chain_up(u, 1)
        chain_down(a, 1)
        chain_up(a, 1)
        reduce_turn(1)
        chain_down(u, 1)
        sum_biases()
        reduce_side(0)
        chain_up(u, 2)
        reduce_turn(0)
        chain_down(u, 2)
        reduce_wait(1)
        write_input_grad()
        chain_end(u)
        sums_start()
        chain_down(a, 2)
        chain_up(a, 2)
        sums_group()
        chain_end(a)
        sums_end()
        reduce_wait(0)
        write_output()
        finish(u)
        finish(a)

    if (gx, na, nm, nz, tiles) == (2, 1, 1, 4, 4):
        tuned_order()
    else:
        any_order()

    for i in range(count):
        for k in range(1, members):
            g_final(i, other_j(k), j).wait_send()
            give_part(i, other_j(k)).wait_send()
        for src in range(nz):
            pl.when((z < nz - 1) & (src <= z))(lambda: send_up(i, src).wait_send())
            pl.when((z > 0) & (src >= z))(lambda: send_down(i, src).wait_send())
            pl.when(src > z)(lambda: g_up(i, src).wait_send())
            pl.when(src < z)(lambda: g_down(i, src).wait_send())
            if gx == 1:
                send_across(i, src, x).wait_send()
                g_across(i, src).wait_send()
    for k in range(1, members):
        own_doc(other_j(k)).wait_send()
    reduce_sent(0)
    reduce_sent(1)
    sums_sent()


def on_device(
    nt,
    n_dp,
    tokens,
    cotangent,
    segments,
    ln_gain,
    ln_bias,
    w_qkv,
    b_qkv,
    w_dense,
    b_dense,
    w_up,
    b_up,
    w_down,
    b_down,
):
    R, D = tokens.shape
    length = segments.shape[1]
    r = w_qkv.shape[0]
    nz = n_dp // 4
    heads = w_qkv.shape[1] // (3 * HEAD)
    gx = 2 if heads % 4 == 0 and 4 * length * D <= 1 << 21 else 1
    members = 2 * gx
    heads = heads // members
    hp = 2 if heads % 2 == 0 else 1
    na = heads // hp
    units = w_up.shape[1] // members
    pw = 512 if units % 512 == 0 else units
    nm = units // pw
    nbuf = gx
    peers, mates = (nz if gx == 2 else 2 * nz), members * nt
    sizes = dict(nt=nt, nz=nz, gx=gx, na=na, nm=nm, hp=hp, length=length, R=R, r=r, pw=pw, nbuf=nbuf)

    widths = ((na, 512), (nm, pw), (nm, pw))
    count = na + 2 * nm
    rows = members * length
    own = D if gx == 2 else D // 2
    chip = 2 * r
    split = D * 3 // 8
    V = pltpu.VMEM
    DMA = pltpu.SemaphoreType.DMA

    def some(shape):
        return V(shape if gx == 2 else (1, 1, 8, 128)[-len(shape) :], BF16)

    scratch = (
        [V((members, na, r, 512), BF16), V((na, 1, 384), F32)]
        + [V((length, 128), F32)] * 2
        + [V((members, 8, length), F32), V((length, 128), F32)]
        + [V((n, D, w), BF16) for n, w in widths]
        + [V((rows, D), BF16), V((rows, D), BF16)]
        + [V((rows, 128), BF16)] * 4
        + [V((na, rows, 128), BF16), V((na, rows, 384), BF16)]
        + [V((length, 128), F32)] * 2
        + [V((nm, rows, pw), BF16), V((nm, rows, pw), F32), V((nm, rows, pw), BF16)]
        + [V((rows, D) if gx == 2 else (8, 128), BF16)]
        + [V((nbuf, gx * length, D), BF16), some((nbuf, nt, R, D - split)), some((nbuf, nt, R, split))]
        + [some((nbuf, R, D)), V((nbuf, nt, R, D), BF16)]
        + [V((n, own, w), F32) for n, w in widths]
        + [V((n, own, w) if gx == 1 else (n, 8, 128), BF16) for _ in range(2) for n, w in widths]
        + [V((n, own, w), BF16) for _ in range(3) for n, w in widths]
        + [V((n, gx * chip, w), BF16) for n, w in widths]
        + [V((n, members, r, w), BF16) for n, w in widths]
        + [V((8, D), F32), V((peers, 8, D), F32), V((mates, 8, D), F32)]
        + [DMA((count,)), DMA((count + 1, members)), DMA((count + 1, members))]
        + [DMA((count, nz))] * 5
        + [DMA((4, nt))] * 2
        + [DMA((4,))] * 2
        + [DMA((4, nt))] * 4
        + [DMA((2, members, nt))] * 2
        + [DMA((count, nz))] * 6
        + [DMA((count, members))] * 2
        + [DMA((2,))] * 2
        + [DMA((peers,))] * 2
        + [DMA((mates,))] * 2
        + [pltpu.SemaphoreType.REGULAR((2,))]
    )
    space = pl.BlockSpec(memory_space=pltpu.VMEM)

    def row(vector):
        return vector.reshape(1, -1)

    args = (
        tokens,
        cotangent,
        segments,
        row(ln_gain),
        row(ln_bias),
        w_qkv,
        row(b_qkv),
        w_dense.T,
        row(b_dense),
        w_up,
        row(b_up),
        w_down.T,
        row(b_down),
    )
    shapes = (
        jax.ShapeDtypeStruct((R, D), BF16),
        jax.ShapeDtypeStruct((R, D), F32),
        jax.ShapeDtypeStruct((1, D), F32),
        jax.ShapeDtypeStruct((1, D), F32),
        jax.ShapeDtypeStruct(w_qkv.shape, F32),
        jax.ShapeDtypeStruct((1, w_qkv.shape[1]), F32),
        jax.ShapeDtypeStruct(w_dense.shape[::-1], F32),
        jax.ShapeDtypeStruct((1, D), F32),
        jax.ShapeDtypeStruct(w_up.shape, F32),
        jax.ShapeDtypeStruct((1, w_up.shape[1]), F32),
        jax.ShapeDtypeStruct(w_down.shape[::-1], F32),
    )
    out = pl.pallas_call(
        functools.partial(kernel, sizes),
        out_shape=shapes,
        in_specs=[space] * len(args),
        out_specs=[space] * len(shapes),
        scratch_shapes=scratch,
        compiler_params=pltpu.CompilerParams(
            collective_id=0, has_side_effects=True, vmem_limit_bytes=67043328
        ),
        name="layer",
    )(*args)
    out = [part.reshape(-1) if part.shape[0] == 1 else part for part in out]
    out[6], out[10] = out[6].T, out[10].T
    return (*out, out[7])


def solution(mesh):
    return jax.shard_map(
        functools.partial(on_device, mesh.shape["tensor"], mesh.shape["dp"]),
        mesh=mesh,
        in_specs=(
            P(("dp", "tensor"), None),
            P(("dp", "tensor"), None),
            P("dp", None),
            P(),
            P(),
            P("dp", "tensor"),
            P("tensor"),
            P("tensor", "dp"),
            P(),
            P("dp", "tensor"),
            P("tensor"),
            P("tensor", "dp"),
            P(),
        ),
        out_specs=(
            P(("dp", "tensor"), None),
            P(("dp", "tensor"), None),
            P(),
            P(),
            P("dp", "tensor"),
            P("tensor"),
            P("tensor", "dp"),
            P(),
            P("dp", "tensor"),
            P("tensor"),
            P("tensor", "dp"),
            P(),
        ),
        check_vma=False,
    )
```

time: 194 us -> 151 us (0.78)
  Pallas kernels: 180 us -> 137 us
    pallas_call x1, Pallas kernels: 180 us -> 137 us  [on_device(): pl.pallas_call(functools.partial(kernel, sizes), out_shape=shapes, in_spe...]
where the time goes in v1:
time: 151 us; the launch traced here: 150 us
  Pallas kernels  137 us (91%)
  local copies, waits for them, and re-layouts  11.2 us (7%)
    pallas_call x1, Pallas kernels, on_device(): pl.pallas_call(functools.partial(kernel, sizes), out_shape=shapes, in_spe...  137 us
    unnamed x29, local copies, waits for them, and re-layouts  9.86 us

profile of v1, /device:TPU:0, one launch (start us, length us, event | category | flops | bytes accessed | tf_op | source)
XLA Modules:
  0.0 150.4 jit_solution(5569333391915456625)
XLA Ops:
  0.6 1.3 reshape.59.b_qkv
  1.9 137.2 %layer.1 = (bf16[256,1024]{1,0:T(8,128)(2,1)}, f32[256,1024]{1,0:T(8,128)}, f32[1,1024]{1,0:T(1,128)}, f32[1,1024]{1,0:T(1,128)}, f32[64,1536]{1,0:T(8,128)}, /*...) custom-call(bf16[256,1024]{1,0:T(8,128)(2,1)} %tokens.1, ...), custom_call_target="tpu_custom_call" | custom-call | tf_op jit(solution)/shard_map/layer/pallas_call | solution.py:1273
  139.1 0.0 copy-start
  139.1 1.4 reduce
  140.5 1.3 copy.36
  141.8 1.9 %copy.37 = bf16[256,1024]{1,0:T(8,128)(2,1)} copy(bf16[256,1024]{1,0:T(8,128)(2,1)} %get-tuple-element.70) | data formatting | bytes 1048576
  143.7 0.0 copy-done
  143.7 1.0 copy.38
  144.6 0.0 copy-done.8
  144.6 0.6 copy.39
  145.2 0.1 copy-done.7
  145.3 0.6 copy.40
  145.9 0.0 copy-done.3
  145.9 0.7 copy.41
  146.7 0.2 copy-done.4
  146.9 0.7 copy.42
  147.6 0.0 copy-done.5
  147.6 0.6 copy.43
  148.2 0.0 copy-done.2
  148.2 0.8 copy.44
  149.0 0.0 copy-done.6
  149.0 0.6 copy.45
  149.6 0.0 copy-done.1
  149.6 0.8 copy.46
  (8 shorter events, 0.0 us)
Async XLA Ops:
  139.1 4.5 %copy-start = (f32[256,1024]{1,0:T(8,128)S(1)}, f32[256,1024]{1,0:T(8,128)}, u32[]{:S(2)}) copy-start(f32[256,1024]{1,0:T(8,128)} %get-tuple-element.71) | copy-start | bytes 3145732
  143.7 1.0 copy-start.8
  143.7 2.3 %copy-start.3 = (f32[64,1536]{1,0:T(8,128)S(1)}, f32[64,1536]{1,0:T(8,128)}, u32[]{:S(2)}) copy-start(f32[64,1536]{1,0:T(8,128)} %get-tuple-element.74) | copy-start | bytes 1179652
  144.6 0.7 copy-start.7
  145.9 1.0 copy-start.4
  145.9 2.3 %copy-start.2 = (f32[64,2048]{1,0:T(8,128)S(1)}, f32[64,2048]{1,0:T(8,128)}, u32[]{:S(2)}) copy-start(f32[64,2048]{1,0:T(8,128)} %get-tuple-element.78) | copy-start | bytes 1572868
  146.9 0.7 copy-start.5
  148.2 0.8 copy-start.6
  148.2 1.4 copy-start.1

commit v2 on v1

--- a/solution.py
+++ b/solution.py
@@ -297,12 +297,17 @@
     acts = (normed, grads)
     tile = min(64, R)
     split = D * 3 // 8
-    left, right = slice(0, split), slice(split, D)
+    over_x, over_t = slice(0, split), slice(split, D)
+    back_split = D // 4
+    back_x, back_t = slice(0, back_split), slice(back_split, D)
 
     def act_rows(jj, tt):
         return rows_at((jj * nt + tt) * R, R)
 
     across_j = c * gx + 1 - x if gx == 2 else c
+    partner_j = (1 - c) * gx + x if gx == 2 else 1 - c
+    far_j = (1 - c) * gx + 1 - x if gx == 2 else 1 - c
+    near = (j, partner_j, across_j, far_j)
 
     def fill_normed():
         def body(n, carry):
@@ -331,23 +336,29 @@
         return copy(b, b, side_send.at[a], side_recv.at[a], across)
 
     def act_corner_x(a, jj, tt):
-        b = acts[a].at[act_rows(jj, tt), left]
+        b = acts[a].at[act_rows(jj, tt), over_x]
         return copy(b, b, corner_x_send.at[a, tt], corner_x_recv.at[a, tt], across)
 
     def act_corner_t(a, tt, src):
-        b = acts[a].at[act_rows(across_j, src), right]
+        b = acts[a].at[act_rows(across_j, src), over_t]
         return copy(b, b, corner_t_send.at[a, tt], corner_t_recv.at[a, src], turned(tt))
 
     def act_pass(a, jj, tt):
         b = acts[a].at[act_rows(jj, tt)]
         return copy(b, b, pass_send.at[a, jj, tt], pass_recv.at[a, jj, tt], partner)
 
-    def act_start(a):
+    def act_start_side(a):
         if gx == 2:
             act_side(a, j).start()
+
+    def act_start_turn(a):
         for k in range(1, nt):
             act_turn(a, other_t(k), t).start()
         act_pass(a, j, t).start()
+
+    def act_start(a):
+        act_start_side(a)
+        act_start_turn(a)
 
     def act_from_turn(a):
         for k in range(1, nt):
@@ -372,10 +383,13 @@
                 act_corner_t(a, t, src).wait_recv()
                 act_pass(a, across_j, src).start()
 
+    def act_wait_of(a, jj):
+        for k in range(nt):
+            act_pass(a, jj, k).wait_recv()
+
     def act_wait(a):
         for xx in range(gx):
-            for k in range(nt):
-                act_pass(a, (1 - c) * gx + xx, k).wait_recv()
+            act_wait_of(a, (1 - c) * gx + xx)
 
     def act_sent(a):
         if gx == 2:
@@ -487,8 +501,14 @@
             return [(0, pw, dot(normed[:, columns], grad_u[i - na], 0, 0))]
         return [(0, pw, dot(grads[:, columns], active[i - na - nm], 0, 0))]
 
+    cut = min(512, own)
+
+    def weight_grad_cut(i, n):
+        at = n * cut if gx == 2 else x * own + n * cut
+        for lo, hi, part in products(i, rows_at(at, cut)):
+            own_of(i)[n * cut : (n + 1) * cut, lo:hi] = part
+
     def weight_grad(i):
-        cut = min(512, own)
         if gx == 1:
             xs = of(xs_a, xs_u, xs_d, i)
             for n in range(own // cut):
@@ -497,9 +517,7 @@
             for to_z in range(nz):
                 g_across(i, to_z).start()
         for n in range(own // cut):
-            at = n * cut if gx == 2 else x * own + n * cut
-            for lo, hi, part in products(i, rows_at(at, cut)):
-                own_of(i)[n * cut : (n + 1) * cut, lo:hi] = part
+            weight_grad_cut(i, n)
 
     def sum_x(i):
         if gx == 1:
@@ -584,7 +602,7 @@
         for k in range(na):
             for part in range(3):
                 ba[k, :, part * 128 : (part + 1) * 128] = pick(
-                    [head_part(b_qkv[...], jj, k, part) for jj in range(members)]
+                    [head_part(b_qkv[...].reshape(1, -1), jj, k, part) for jj in range(members)]
                 )
         steps = np.arange(ROT // 2, dtype=np.float32) * 2.0 / ROT
         inverse = (np.float32(ROTARY_BASE) ** -steps).astype(np.float32)
@@ -603,15 +621,14 @@
 
         lax.fori_loop(0, length // 128, table, 0)
 
-    lanes_of_doc = 128 // members
-
     def prepare_docs():
         for k in range(1, members):
             doc_of(other_j(k)).wait_recv()
-        for n in range(length // 128):
-            cut = slice(n * 128, (n + 1) * 128)
-            rows = [jnp.broadcast_to(docs[s, 0:1, cut], (lanes_of_doc, 128)) for s in range(members)]
-            doc_column[cut, :] = jnp.transpose(jnp.concatenate(rows, axis=0))
+        for s in range(members):
+            for n in range(length // 128):
+                cut = slice(n * 128, (n + 1) * 128)
+                rows = jnp.broadcast_to(docs[s, 0:1, cut], (128, 128))
+                doc_column[s, cut, :] = jnp.transpose(rows).astype(BF16)
 
     RT = min(512, total_rows)
     tiles = total_rows // RT
@@ -673,8 +690,8 @@
             grad_p = dot(g, values, 1, 1)
             at = k_at + lax.broadcasted_iota(jnp.int32, (block, window), 1)
             here = q_at + lax.broadcasted_iota(jnp.int32, (block, window), 0)
-            lane = s * lanes_of_doc
-            same = doc_column[pl.ds(q_at, block), lane : lane + 1] == docs[s, 0:1, pl.ds(k_at, window)]
+            own_doc_of = doc_column[s, pl.ds(q_at, block), 0:1].astype(F32)
+            same = own_doc_of == docs[s, 0:1, pl.ds(k_at, window)]
             allowed = same & (at <= here)
             probs, grad_s = [], []
             for h in range(hp):
@@ -713,12 +730,11 @@
         rows = rows_at(n * RT, RT)
         grad_u[k, rows, :] = (dot(grads[rows, :], wd[k], 1, 0) * slope[k, rows, :]).astype(BF16)
 
-    per_core = gx * length
-    HT = min(512, per_core)
-
-    def branch_rows(a, cc):
+    HT = min(512, length)
+
+    def branch(a, jj):
         def body(n, carry):
-            rows = rows_at(cc * per_core + n * HT, HT)
+            rows = rows_at(jj * length + n * HT, HT)
             total = None
             for k in range(na):
                 if a == 0:
@@ -735,20 +751,30 @@
             partials[a][rows, :] = total.astype(BF16)
             return carry
 
-        lax.fori_loop(0, per_core // HT, body, 0)
-
-    def half_copy(a, cc):
-        rows = rows_at(cc * per_core, per_core)
-        return copy(partials[a].at[rows], core_in.at[a % nbuf], half_send.at[a], half_recv.at[a], partner)
-
-    def branches_give(a):
-        branch_rows(a, 1 - c)
-        if nbuf == 1 and a == second:
-            pl.semaphore_wait(credit.at[0], 1)
-        half_copy(a, 1 - c).start()
-
-    def branches_keep(a):
-        branch_rows(a, c)
+        lax.fori_loop(0, length // HT, body, 0)
+
+    def half_copy(a, jj):
+        at = jj - (1 - c) * gx
+        return copy(
+            partials[a].at[rows_at(jj * length, length)],
+            core_in.at[a % nbuf, rows_at(at * length, length)],
+            half_send.at[a, at],
+            half_recv.at[a, at],
+            partner,
+        )
+
+    def branch_give(a, jj):
+        branch(a, jj)
+        half_copy(a, jj).start()
+
+    def branches(a):
+        for n, jj in enumerate((far_j, partner_j)[2 - gx :]):
+            branch(a, jj)
+            if n == 0 and nbuf == 1 and a == second:
+                pl.semaphore_wait(credit.at[0], 1)
+            half_copy(a, jj).start()
+        for jj in (across_j, j)[2 - gx :]:
+            branch(a, jj)
 
     def block_rows(jj, tt):
         return rows_at((jj * nt + tt) * R, R)
@@ -763,11 +789,11 @@
         )
 
     def corner_t_copy(a, tt, src):
-        b = partials[a].at[block_rows(across_j, tt), left]
+        b = partials[a].at[block_rows(across_j, tt), back_t]
         return copy(b, corner_t.at[a % nbuf, src], corner_t_send.at[2 + a, tt], corner_t_recv.at[2 + a, src], turned(tt))
 
     def corner_x_copy(a, jj, tt):
-        b = partials[a].at[block_rows(jj, tt), right]
+        b = partials[a].at[block_rows(jj, tt), back_x]
         return copy(b, corner_x.at[a % nbuf, tt], corner_x_send.at[2 + a, tt], corner_x_recv.at[2 + a, tt], across)
 
     def side_copy(a, jj):
@@ -779,8 +805,8 @@
         return copy(b, side_t.at[a % nbuf, src], turn_send.at[2 + a, tt], turn_recv.at[2 + a, src], turned(tt))
 
     def reduce_corner(a):
-        half_copy(a, 1 - c).wait_recv()
         if gx == 2:
+            half_copy(a, far_j).wait_recv()
             for k in range(1, nt):
                 tt = other_t(k)
                 partials[a][block_rows(across_j, tt), :] = both_cores(a, across_j, tt).astype(BF16)
@@ -789,24 +815,25 @@
 
     def reduce_side(a):
         if gx == 2:
-            total = both_cores(a, across_j, t, left)
+            total = both_cores(a, across_j, t, back_t)
             for k in range(1, nt):
                 corner_t_copy(a, t, other_t(k)).wait_recv()
                 total = total + corner_t[a % nbuf, other_t(k)].astype(F32)
-            partials[a][block_rows(across_j, t), left] = total.astype(BF16)
-            partials[a][block_rows(across_j, t), right] = both_cores(a, across_j, t, right).astype(BF16)
+            partials[a][block_rows(across_j, t), back_t] = total.astype(BF16)
+            partials[a][block_rows(across_j, t), back_x] = both_cores(a, across_j, t, back_x).astype(BF16)
             side_copy(a, across_j).start()
 
     def reduce_turn(a):
         if nbuf == 1 and a == second and nt > 1:
             pl.semaphore_wait(credit.at[1], nt - 1)
+        half_copy(a, partner_j).wait_recv()
         for k in range(1, nt):
             tt = other_t(k)
             if gx == 2:
                 corner_x_copy(a, j, tt).wait_recv()
-                total = both_cores(a, j, tt, right) + corner_x[a % nbuf, tt].astype(F32)
-                partials[a][block_rows(j, tt), right] = total.astype(BF16)
-                partials[a][block_rows(j, tt), left] = both_cores(a, j, tt, left).astype(BF16)
+                total = both_cores(a, j, tt, back_x) + corner_x[a % nbuf, tt].astype(F32)
+                partials[a][block_rows(j, tt), back_x] = total.astype(BF16)
+                partials[a][block_rows(j, tt), back_t] = both_cores(a, j, tt, back_t).astype(BF16)
             else:
                 partials[a][block_rows(j, tt), :] = both_cores(a, j, tt).astype(BF16)
             turn_copy(a, tt, t).start()
@@ -829,7 +856,8 @@
         return restore(total)
 
     def reduce_sent(a):
-        half_copy(a, 1 - c).wait_send()
+        for xx in range(gx):
+            half_copy(a, (1 - c) * gx + xx).wait_send()
         if gx == 2:
             side_copy(a, across_j).wait_send()
         for k in range(1, nt):
@@ -1002,8 +1030,7 @@
         act_sent(1)
         sum_biases()
         for a in (1, 0) if gx == 2 else (0, 1):
-            branches_give(a)
-            branches_keep(a)
+            branches(a)
             reduce_corner(a)
             if a != second:
                 chains(U, 0, nz - 1)
@@ -1029,113 +1056,127 @@
 
     def tuned_order():
         (a,), (u,), (d,) = A, U, Dn
+        stage()
+        fill_grads()
         fill_normed()
-        stage()
         enter()
-        share(u)
         share(a)
         give_docs()
-        fill_grads()
+        share(u)
+        act_start_turn(0)
+        act_start_side(0)
+        act_start_side(1)
+        send_own(a)
+        act_start_turn(1)
+        share(d)
+        prepare()
         send_own(u)
-        act_start(0)
-        send_own(a)
+        forward_up(a, 1)
+        forward_down(a, 1)
+        act_from_turn(0)
+        act_from_side(0)
         forward_up(u, 1)
         forward_down(u, 1)
-        act_start(1)
-        act_from_side(0)
-        forward_down(a, 1)
-        act_from_turn(0)
-        forward_up(a, 1)
-        share(d)
+        act_wait_of(0, partner_j)
+        forward_up(a, 2)
+        act_from_turn(1)
+        forward_up(u, 2)
+        forward_down(a, 2)
+        act_from_side(1)
         forward_down(u, 2)
-        forward_down(a, 2)
-        forward_up(u, 2)
-        act_from_side(1)
-        act_from_turn(1)
-        forward_up(a, 2)
         prepare_docs()
+        send_own(d)
+        act_wait_of(1, partner_j)
+        forward_up(a, 3)
+        forward_down(a, 3)
+        project(0, partner_j)
+        project_back(0, partner_j)
+        attend(0, partner_j)
         act_finish(0)
+        project(0, across_j)
+        project_back(0, j)
+        project(0, j)
+        forward_down(u, 3)
         forward_up(u, 3)
-        act_wait(0)
-        forward_down(u, 3)
-        hidden(0, 1)
-        prepare()
-        send_own(d)
-        hidden(0, 2)
-        forward_down(a, 3)
-        forward_up(a, 3)
-        project(0, 0)
-        hidden(0, 3)
-        project(0, 2)
-        project(0, 3)
-        hidden(0, 0)
+        hidden(0, across_j)
+        hidden(0, j)
+        act_wait_of(0, far_j)
+        hidden(0, partner_j)
         act_finish(1)
-        project(0, 1)
-        act_wait(1)
-        weight_grad(d)
+        hidden(0, far_j)
+        project(0, far_j)
+        project_back(0, across_j)
+        act_wait_of(1, far_j)
+        weight_grad_cut(d, 1)
+        forward_down(d, 1)
         chain_up(d, 0)
+        forward_up(d, 1)
+        weight_grad_cut(d, 0)
         chain_down(d, 0)
-        forward_up(d, 1)
-        forward_down(d, 1)
-        each_tile(project_back, 0)
-        attend(0, 0)
-        attend(0, 1)
+        attend(0, j)
+        attend(0, across_j)
         forward_up(d, 2)
+        forward_down(d, 2)
+        project_back(0, far_j)
+        chain_up(d, 1)
         chain_down(d, 1)
-        forward_down(d, 2)
-        chain_up(d, 1)
-        attend(0, 3)
-        attend(0, 2)
-        weight_grad(a)
+        attend(0, far_j)
+        weight_grad_cut(a, 0)
+        forward_up(d, 3)
         forward_down(d, 3)
-        forward_up(d, 3)
+        hidden_back(0, far_j)
+        branch_give(1, far_j)
+        chain_up(d, 2)
         chain_down(d, 2)
-        chain_up(d, 2)
-        hidden_back(0, 2)
-        hidden_back(0, 0)
-        hidden_back(0, 3)
-        hidden_back(0, 1)
-        weight_grad(u)
+        hidden_back(0, across_j)
+        branch(1, across_j)
+        reduce_corner(1)
+        weight_grad_cut(a, 1)
+        chain_down(a, 0)
         chain_up(a, 0)
-        branches_give(1)
-        chain_down(a, 0)
         act_sent(0)
         act_sent(1)
-        branches_give(0)
+        branch_give(0, far_j)
+        branch(0, across_j)
+        hidden_back(0, j)
+        hidden_back(0, partner_j)
+        reduce_corner(0)
+        weight_grad_cut(u, 0)
+        chain_down(u, 0)
+        weight_grad_cut(u, 1)
+        chain_up(u, 0)
         chain_end(d)
-        branches_keep(1)
-        reduce_corner(1)
-        chain_down(u, 0)
-        branches_keep(0)
-        chain_up(u, 0)
-        reduce_corner(0)
-        finish(d)
+        chain_up(a, 1)
+        branch_give(1, partner_j)
         reduce_side(1)
+        branch(0, j)
+        branch(1, j)
         chain_up(u, 1)
         chain_down(a, 1)
-        chain_up(a, 1)
         reduce_turn(1)
+        branch_give(0, partner_j)
         chain_down(u, 1)
         sum_biases()
+        chain_up(a, 2)
+        reduce_turn(0)
+        chain_down(a, 2)
         reduce_side(0)
-        chain_up(u, 2)
-        reduce_turn(0)
-        chain_down(u, 2)
         reduce_wait(1)
         write_input_grad()
+        sums_start()
+        chain_down(u, 2)
+        chain_up(u, 2)
+        chain_end(a)
+        sums_group()
+        finish(d)
+        finish(a)
         chain_end(u)
-        sums_start()
-        chain_down(a, 2)
-        chain_up(a, 2)
-        sums_group()
-        chain_end(a)
-        sums_end()
         reduce_wait(0)
         write_output()
+        sums_end()
         finish(u)
-        finish(a)
-
-    if (gx, na, nm, nz, tiles) == (2, 1, 1, 4, 4):
+
+    if (gx, na, nm, nz, tiles, RT) == (2, 1, 1, 4, 4, length):
         tuned_order()
     else:
         any_order()
@@ -1157,6 +1198,44 @@
     reduce_sent(0)
     reduce_sent(1)
     sums_sent()
+
+
+def hand_out(arrays):
+    wide = [n for n, array in enumerate(arrays) if array.shape[0] > 1]
+    thin = [n for n, array in enumerate(arrays) if array.shape[0] == 1]
+
+    def body(*refs):
+        count = len(arrays)
+        given, taken, buffers, sems = refs[:count], refs[count : 2 * count], refs[2 * count : -1], refs[-1]
+        reads = [pltpu.make_async_copy(given[n], buffers[i], sems.at[0, i]) for i, n in enumerate(wide)]
+        writes = [pltpu.make_async_copy(buffers[i], taken[n], sems.at[1, i]) for i, n in enumerate(wide)]
+        for read in reads:
+            read.start()
+        for n in thin:
+            taken[n][...] = given[n][0]
+        for read, write in zip(reads, writes):
+            read.wait()
+            write.start()
+        for write in writes:
+            write.wait()
+
+    def specs():
+        return [pl.BlockSpec(memory_space=pltpu.VMEM if n in thin else pl.ANY) for n in range(len(arrays))]
+
+    return list(
+        pl.pallas_call(
+            body,
+            out_shape=[
+                jax.ShapeDtypeStruct(array.shape[1:] if n in thin else array.shape, array.dtype)
+                for n, array in enumerate(arrays)
+            ],
+            in_specs=specs(),
+            out_specs=specs(),
+            scratch_shapes=[pltpu.VMEM(arrays[n].shape, arrays[n].dtype) for n in wide]
+            + [pltpu.SemaphoreType.DMA((2, len(wide)))],
+            name="hand_out",
+        )(*arrays)
+    )
 
 
 def on_device(
@@ -1198,7 +1277,7 @@
     rows = members * length
     own = D if gx == 2 else D // 2
     chip = 2 * r
-    split = D * 3 // 8
+    split = D // 4
     V = pltpu.VMEM
     DMA = pltpu.SemaphoreType.DMA
 
@@ -1208,7 +1287,7 @@
     scratch = (
         [V((members, na, r, 512), BF16), V((na, 1, 384), F32)]
         + [V((length, 128), F32)] * 2
-        + [V((members, 8, length), F32), V((length, 128), F32)]
+        + [V((members, 8, length), F32), V((members, length, 128), BF16)]
         + [V((n, D, w), BF16) for n, w in widths]
         + [V((rows, D), BF16), V((rows, D), BF16)]
         + [V((rows, 128), BF16)] * 4
@@ -1216,7 +1295,7 @@
         + [V((length, 128), F32)] * 2
         + [V((nm, rows, pw), BF16), V((nm, rows, pw), F32), V((nm, rows, pw), BF16)]
         + [V((rows, D) if gx == 2 else (8, 128), BF16)]
-        + [V((nbuf, gx * length, D), BF16), some((nbuf, nt, R, D - split)), some((nbuf, nt, R, split))]
+        + [V((nbuf, gx * length, D), BF16), some((nbuf, nt, R, split)), some((nbuf, nt, R, D - split))]
         + [some((nbuf, R, D)), V((nbuf, nt, R, D), BF16)]
         + [V((n, own, w), F32) for n, w in widths]
         + [V((n, own, w) if gx == 1 else (n, 8, 128), BF16) for _ in range(2) for n, w in widths]
@@ -1232,7 +1311,7 @@
         + [DMA((2, members, nt))] * 2
         + [DMA((count, nz))] * 6
         + [DMA((count, members))] * 2
-        + [DMA((2,))] * 2
+        + [DMA((2, gx))] * 2
         + [DMA((peers,))] * 2
         + [DMA((mates,))] * 2
         + [pltpu.SemaphoreType.REGULAR((2,))]
@@ -1249,7 +1328,7 @@
         row(ln_gain),
         row(ln_bias),
         w_qkv,
-        row(b_qkv),
+        b_qkv,
         w_dense.T,
         row(b_dense),
         w_up,
@@ -1281,9 +1360,9 @@
         ),
         name="layer",
     )(*args)
-    out = [part.reshape(-1) if part.shape[0] == 1 else part for part in out]
+    out = hand_out((*out, out[7]))
     out[6], out[10] = out[6].T, out[10].T
-    return (*out, out[7])
+    return tuple(out)
 
 
 def solution(mesh):

time: 151 us -> 129 us (0.85)
  local copies, waits for them, and re-layouts: 11.2 us -> 0 us
  Pallas kernels: 137 us -> 128 us
    pallas_call x1, Pallas kernels: 137 us -> 124 us  [on_device(): pl.pallas_call(functools.partial(kernel, sizes), out_shape=shapes, in_spe...]
    unnamed x29 -> x0, local copies, waits for them, and re-layouts: 9.86 us -> none
    pallas_call x0 -> x1, Pallas kernels: none -> 4.37 us  [hand_out(): pl.pallas_call(body, out_shape=[jax.ShapeDtypeStruct(array.shape[1:] if n...]
where the time goes in v2:
time: 129 us
  Pallas kernels  128 us (99%)
    pallas_call x1, Pallas kernels, on_device(): pl.pallas_call(functools.partial(kernel, sizes), out_shape=shapes, in_spe...  124 us
    pallas_call x1, Pallas kernels, hand_out(): pl.pallas_call(body, out_shape=[jax.ShapeDtypeStruct(array.shape[1:] if n...  4.37 us

profile of v2, /device:TPU:0, one launch (start us, length us, event | category | flops | bytes accessed | tf_op | source)
XLA Modules:
  0.0 128.7 jit_solution(8651672959592106261)
XLA Ops:
  0.6 123.5 %layer.1 = (bf16[256,1024]{1,0:T(8,128)(2,1)}, f32[256,1024]{1,0:T(8,128)}, f32[1,1024]{1,0:T(1,128)}, f32[1,1024]{1,0:T(1,128)}, f32[64,1536]{1,0:T(8,128)}, /*...) custom-call(bf16[256,1024]{1,0:T(8,128)(2,1)} %tokens.1, ...), custom_call_target="tpu_custom_call" | custom-call | tf_op jit(solution)/shard_map/layer/pallas_call | solution.py:1352
  124.2 4.4 %hand_out.1 = (bf16[256,1024]{1,0:T(8,128)(2,1)}, f32[256,1024]{1,0:T(8,128)}, f32[1024]{0:T(1024)}, f32[1024]{0:T(1024)}, f32[64,1536]{1,0:T(8,128)}, /*index=5...) custom-call(bf16[256,1024]{1,0:T(8,128)(2,1)} %get-tuple-element.35., ...), custom_call_target="tpu_custom_call" | custom-call | tf_op jit(solution)/shard_map/hand_out/pallas_call | solution.py:1226

commit v3 on v2

--- a/solution.py
+++ b/solution.py
@@ -36,29 +36,39 @@
 
 def kernel(
     sizes,
-    tokens,
-    cotangent,
+    tokens_hbm,
+    cotangent_hbm,
     segments,
     gain,
     shift,
-    w_qkv,
+    w_qkv_hbm,
     b_qkv,
-    w_dense,
+    w_dense_hbm,
     b_dense,
     w_up,
     b_up,
     w_down,
     b_down,
+    output_hbm,
+    input_grad_hbm,
+    gain_grad,
+    shift_grad,
+    qkv_grad_hbm,
+    qkv_bias,
+    dense_grad_hbm,
+    dense_bias,
+    up_grad_hbm,
+    up_bias,
+    down_grad_hbm,
+    tokens,
+    cotangent,
+    w_qkv,
+    w_dense,
     output,
     input_grad,
-    gain_grad,
-    shift_grad,
     qkv_grad,
-    qkv_bias,
     dense_grad,
-    dense_bias,
     up_grad,
-    up_bias,
     down_grad,
     wa_in,
     ba,
@@ -116,6 +126,7 @@
     vec_z,
     vec_m,
     local_sem,
+    io_sem,
     share_send,
     share_recv,
     up_send,
@@ -217,20 +228,43 @@
 
     barrier = pltpu.get_barrier_semaphore()
     greeted = [member(other_j(k)) for k in range(1, members)] + ([] if gx == 2 else [across])
-    if gx == 1:
-        greeted += [device(other_z(k), 1 - x, c, t) for k in range(1, nz)]
-    if nt > 1:
-        greeted += [
-            device(z, jj % 2 if gx == 2 else x, jj // 2 if gx == 2 else jj, other_t(k))
-            for k in range(1, nt)
-            for jj in [other_j(n) for n in range(1, members)]
-        ]
-    greeted += [along(other_z(k)) for k in range(1, nz)] + [turned(other_t(k)) for k in range(1, nt)]
+    greeted += [
+        device(z, jj % 2 if gx == 2 else x, jj // 2 if gx == 2 else jj, other_t(k))
+        for k in range(1, nt)
+        for jj in [other_j(n) for n in range(members)]
+    ]
+
+    def greet(other):
+        pl.semaphore_signal(barrier, inc=1, device_id=other, device_id_type=MESH)
+
     for other in greeted:
-        pl.semaphore_signal(barrier, inc=1, device_id=other, device_id_type=MESH)
+        greet(other)
+    pl.when(z > 0)(lambda: greet(along(z - 1)))
+    pl.when(z < nz - 1)(lambda: greet(along(z + 1)))
+
+    reads = [
+        pltpu.make_async_copy(src, dst, io_sem.at[n])
+        for n, (src, dst) in enumerate(
+            ((w_qkv_hbm, w_qkv), (w_dense_hbm, w_dense), (tokens_hbm, tokens), (cotangent_hbm, cotangent))
+        )
+    ]
+    for read in reads:
+        read.start()
 
     def enter():
-        pl.semaphore_wait(barrier, len(greeted))
+        pl.semaphore_wait(barrier, len(greeted) + jnp.minimum(z, 1) + jnp.minimum(nz - 1 - z, 1))
+
+    results = (
+        (output, output_hbm),
+        (input_grad, input_grad_hbm),
+        (qkv_grad, qkv_grad_hbm),
+        (dense_grad, dense_grad_hbm),
+        (up_grad, up_grad_hbm),
+        (down_grad, down_grad_hbm),
+    )
+
+    def result(n):
+        return pltpu.make_async_copy(*results[n], io_sem.at[4 + n])
 
     def part_of(i, jj):
         if i in A:
@@ -245,9 +279,11 @@
         dst = weights(i).at[own_rows]
         return copy(part_of(i, jj), dst, share_send.at[i, jj], share_recv.at[i, j], member(jj))
 
+    def member_rows(jj):
+        return rows_at(z * zb + (jj % 2 * 2 + jj // 2) * r if gx == 2 else (x * nz + z) * chip + jj * r, r)
+
     def take_part(i, jj):
-        at = z * zb + (jj % 2 * 2 + jj // 2) * r if gx == 2 else (x * nz + z) * chip + jj * r
-        dst = weights(i).at[rows_at(at, r)]
+        dst = weights(i).at[member_rows(jj)]
         return copy(part_of(i, j), dst, share_send.at[i, jj], share_recv.at[i, jj], member(jj))
 
     def share(i):
@@ -266,6 +302,8 @@
         return copy(docs.at[jj], docs.at[jj], share_send.at[count, jj], share_recv.at[count, jj], member(jj))
 
     def stage():
+        reads[0].wait()
+        reads[1].wait()
         for jj in range(members):
             for k in range(na):
                 for part in range(3):
@@ -310,6 +348,8 @@
     near = (j, partner_j, across_j, far_j)
 
     def fill_normed():
+        reads[2].wait()
+
         def body(n, carry):
             rows = rows_at(n * tile, tile)
             normal, _ = normalize(tokens[rows, :].astype(F32))
@@ -321,6 +361,8 @@
         lax.fori_loop(0, R // tile, body, 0)
 
     def fill_grads():
+        reads[3].wait()
+
         def body(n, carry):
             grads[rows_at((j * nt + t) * R + n * tile, tile), :] = permute(cotangent[rows_at(n * tile, tile), :])
             return carry
@@ -418,12 +460,25 @@
         b = weights(i).at[rows_at((xx * nz + src) * chip, chip)]
         return copy(b, b, x_send.at[i, src], x_recv.at[i, src], across)
 
+    def send_first(i):
+        def along_z(sems, to):
+            return copy(part_of(i, j), weights(i).at[own_rows], sems.at[i, z], z_recv.at[i, z], to)
+
+        pl.when(z < nz - 1)(lambda: along_z(up_send, along(z + 1)).start())
+        pl.when(z > 0)(lambda: along_z(down_send, along(z - 1)).start())
+
     def send_own(i):
         local_copy(i).wait()
         for k in range(1, members):
-            take_part(i, other_j(k)).wait_recv()
-        pl.when(z < nz - 1)(lambda: send_up(i, z).start())
-        pl.when(z > 0)(lambda: send_down(i, z).start())
+            jj = other_j(k)
+            take_part(i, jj).wait_recv()
+            rows = weights(i).at[member_rows(jj)]
+
+            def along_z(sems, to):
+                return copy(rows, rows, sems.at[i, z], z_recv.at[i, z], to)
+
+            pl.when(z < nz - 1)(lambda: along_z(up_send, along(z + 1)).start())
+            pl.when(z > 0)(lambda: along_z(down_send, along(z - 1)).start())
         if gx == 1:
             send_across(i, z, x).start()
 
@@ -591,6 +646,11 @@
             else:
                 out, k = (up_grad, i - na) if i in U else (down_grad, i - na - nm)
                 out[:, jj * units + k * pw : jj * units + (k + 1) * pw] = part
+        if i == A[-1]:
+            result(2).start()
+            result(3).start()
+        if i in (U[-1], Dn[-1]):
+            result(4 if i in U else 5).start()
 
     def pick(parts):
         total = parts[0]
@@ -881,14 +941,25 @@
             return carry
 
         lax.fori_loop(0, R // tile, body, 0)
+        result(0).start()
+
+    def put(row, at, values):
+        end = at + values.shape[1]
+        for h in range(2):
+            lo, hi = max(at, h * D // 2), min(end, (h + 1) * D // 2)
+            if lo < hi:
+                cols = slice(lo - h * D // 2, hi - h * D // 2)
+                vec[2 * row + h : 2 * row + h + 1, cols] += values[:, lo - at : hi - at]
+
+    def taken(array, row):
+        return jnp.concatenate([array[2 * row : 2 * row + 1], array[2 * row + 1 : 2 * row + 2]], axis=1)
 
     def sum_biases():
         vec[...] = jnp.zeros_like(vec)
         for k in range(nm):
-            vec[3:4, k * pw : (k + 1) * pw] = jnp.sum(grad_u[k].astype(F32), axis=0, keepdims=True)
+            put(3, k * pw, jnp.sum(grad_u[k].astype(F32), axis=0, keepdims=True))
         for k in range(na):
-            at = units + k * 384
-            vec[3:4, at : at + 384] = jnp.sum(grad_z[k].astype(F32), axis=0, keepdims=True)
+            put(3, units + k * 384, jnp.sum(grad_z[k].astype(F32), axis=0, keepdims=True))
 
     def write_input_grad():
         def body(n, carry):
@@ -896,9 +967,9 @@
             normal, inverse = normalize(tokens[rows, :].astype(F32))
             up = cotangent[rows, :].astype(F32)
             grad = reduced(1, n)
-            vec[0:1, :] += jnp.sum(grad * normal, axis=0, keepdims=True)
-            vec[1:2, :] += jnp.sum(grad, axis=0, keepdims=True)
-            vec[2:3, :] += jnp.sum(up, axis=0, keepdims=True)
+            put(0, 0, jnp.sum(grad * normal, axis=0, keepdims=True))
+            put(1, 0, jnp.sum(grad, axis=0, keepdims=True))
+            put(2, 0, jnp.sum(up, axis=0, keepdims=True))
             scaled = grad * gain[...]
             input_grad[rows, :] = up + inverse * (
                 scaled
@@ -908,6 +979,7 @@
             return carry
 
         lax.fori_loop(0, R // tile, body, 0)
+        result(1).start()
 
     peers = nz if gx == 2 else 2 * nz
     mates = members * nt
@@ -944,11 +1016,11 @@
         total = vec_m[0]
         for k in range(1, mates):
             total = total + vec_m[k]
-        gain_grad[...] = total[0:1]
-        shift_grad[...] = total[1:2]
-        dense_bias[...] = total[2:3]
+        gain_grad[...] = taken(total, 0)
+        shift_grad[...] = taken(total, 1)
+        dense_bias[...] = taken(total, 2)
         for jj in range(members):
-            row = vec_m[jj * nt + t][3:4]
+            row = taken(vec_m[jj * nt + t], 3)
             up_bias[:, jj * units : (jj + 1) * units] = row[:, :units]
             for k in range(na):
                 part = row[:, units + k * 384 : units + (k + 1) * 384]
@@ -981,6 +1053,7 @@
         fill_normed()
         enter()
         for i in U + A + Dn:
+            send_first(i)
             share(i)
         give_docs()
         act_start(0)
@@ -1057,110 +1130,114 @@
     def tuned_order():
         (a,), (u,), (d,) = A, U, Dn
         stage()
-        fill_grads()
-        fill_normed()
         enter()
         share(a)
         give_docs()
+        send_first(d)
+        fill_normed()
+        send_first(u)
         share(u)
+        prepare()
+        send_first(a)
+        fill_grads()
         act_start_turn(0)
+        send_own(a)
         act_start_side(0)
         act_start_side(1)
-        send_own(a)
         act_start_turn(1)
-        share(d)
-        prepare()
         send_own(u)
         forward_up(a, 1)
+        share(d)
         forward_down(a, 1)
+        forward_down(u, 1)
+        forward_down(a, 2)
+        forward_up(u, 1)
+        prepare_docs()
+        forward_up(a, 2)
         act_from_turn(0)
         act_from_side(0)
-        forward_up(u, 1)
-        forward_down(u, 1)
         act_wait_of(0, partner_j)
-        forward_up(a, 2)
-        act_from_turn(1)
+        forward_down(u, 2)
         forward_up(u, 2)
-        forward_down(a, 2)
-        act_from_side(1)
-        forward_down(u, 2)
-        prepare_docs()
-        send_own(d)
-        act_wait_of(1, partner_j)
         forward_up(a, 3)
         forward_down(a, 3)
+        act_from_side(1)
+        act_from_turn(1)
         project(0, partner_j)
-        project_back(0, partner_j)
-        attend(0, partner_j)
-        act_finish(0)
-        project(0, across_j)
+        send_own(d)
         project_back(0, j)
         project(0, j)
+        attend(0, j)
+        act_wait_of(1, partner_j)
+        act_finish(0)
         forward_down(u, 3)
         forward_up(u, 3)
         hidden(0, across_j)
         hidden(0, j)
         act_wait_of(0, far_j)
         hidden(0, partner_j)
+        hidden(0, far_j)
         act_finish(1)
-        hidden(0, far_j)
+        forward_up(d, 1)
+        forward_down(d, 1)
+        project(0, across_j)
         project(0, far_j)
-        project_back(0, across_j)
         act_wait_of(1, far_j)
-        weight_grad_cut(d, 1)
-        forward_down(d, 1)
-        chain_up(d, 0)
-        forward_up(d, 1)
         weight_grad_cut(d, 0)
         chain_down(d, 0)
-        attend(0, j)
-        attend(0, across_j)
+        weight_grad_cut(d, 1)
+        chain_up(d, 0)
+        project_back(0, far_j)
+        attend(0, far_j)
+        project_back(0, across_j)
         forward_up(d, 2)
         forward_down(d, 2)
-        project_back(0, far_j)
+        attend(0, across_j)
+        chain_down(d, 1)
+        project_back(0, partner_j)
         chain_up(d, 1)
-        chain_down(d, 1)
-        attend(0, far_j)
-        weight_grad_cut(a, 0)
+        attend(0, partner_j)
+        forward_down(d, 3)
         forward_up(d, 3)
-        forward_down(d, 3)
         hidden_back(0, far_j)
         branch_give(1, far_j)
+        hidden_back(0, across_j)
+        chain_down(d, 2)
         chain_up(d, 2)
-        chain_down(d, 2)
-        hidden_back(0, across_j)
         branch(1, across_j)
         reduce_corner(1)
+        weight_grad_cut(a, 0)
         weight_grad_cut(a, 1)
         chain_down(a, 0)
         chain_up(a, 0)
         act_sent(0)
         act_sent(1)
         branch_give(0, far_j)
-        branch(0, across_j)
         hidden_back(0, j)
         hidden_back(0, partner_j)
+        branch(0, across_j)
+        weight_grad_cut(u, 0)
         reduce_corner(0)
-        weight_grad_cut(u, 0)
         chain_down(u, 0)
         weight_grad_cut(u, 1)
         chain_up(u, 0)
+        sum_biases()
         chain_end(d)
         chain_up(a, 1)
+        reduce_side(1)
+        branch(1, j)
         branch_give(1, partner_j)
-        reduce_side(1)
+        chain_down(a, 1)
         branch(0, j)
-        branch(1, j)
-        chain_up(u, 1)
-        chain_down(a, 1)
         reduce_turn(1)
         branch_give(0, partner_j)
+        chain_up(u, 1)
         chain_down(u, 1)
-        sum_biases()
+        finish(d)
+        reduce_side(0)
+        reduce_turn(0)
         chain_up(a, 2)
-        reduce_turn(0)
         chain_down(a, 2)
-        reduce_side(0)
         reduce_wait(1)
         write_input_grad()
         sums_start()
@@ -1168,12 +1245,11 @@
         chain_up(u, 2)
         chain_end(a)
         sums_group()
-        finish(d)
-        finish(a)
         chain_end(u)
+        sums_end()
         reduce_wait(0)
         write_output()
-        sums_end()
+        finish(a)
         finish(u)
 
     if (gx, na, nm, nz, tiles, RT) == (2, 1, 1, 4, 4, length):
@@ -1198,6 +1274,8 @@
     reduce_sent(0)
     reduce_sent(1)
     sums_sent()
+    for n in range(len(results)):
+        result(n).wait()
 
 
 def hand_out(arrays):
@@ -1302,8 +1380,8 @@
         + [V((n, own, w), BF16) for _ in range(3) for n, w in widths]
         + [V((n, gx * chip, w), BF16) for n, w in widths]
         + [V((n, members, r, w), BF16) for n, w in widths]
-        + [V((8, D), F32), V((peers, 8, D), F32), V((mates, 8, D), F32)]
-        + [DMA((count,)), DMA((count + 1, members)), DMA((count + 1, members))]
+        + [V((8, D // 2), F32), V((peers, 8, D // 2), F32), V((mates, 8, D // 2), F32)]
+        + [DMA((count,)), DMA((10,)), DMA((count + 1, members)), DMA((count + 1, members))]
         + [DMA((count, nz))] * 5
         + [DMA((4, nt))] * 2
         + [DMA((4,))] * 2
@@ -1316,7 +1394,7 @@
         + [DMA((mates,))] * 2
         + [pltpu.SemaphoreType.REGULAR((2,))]
     )
-    space = pl.BlockSpec(memory_space=pltpu.VMEM)
+    space, far = pl.BlockSpec(memory_space=pltpu.VMEM), pl.BlockSpec(memory_space=pl.ANY)
 
     def row(vector):
         return vector.reshape(1, -1)
@@ -1352,9 +1430,11 @@
     out = pl.pallas_call(
         functools.partial(kernel, sizes),
         out_shape=shapes,
-        in_specs=[space] * len(args),
-        out_specs=[space] * len(shapes),
-        scratch_shapes=scratch,
+        in_specs=[far if n in (0, 1, 5, 7, 9, 11) else space for n in range(len(args))],
+        out_specs=[space if n in (2, 3, 5, 7, 9) else far for n in range(len(shapes))],
+        scratch_shapes=[V(args[n].shape, BF16) for n in (0, 1, 5, 7)]
+        + [V(shapes[n].shape, shapes[n].dtype) for n in (0, 1, 4, 6, 8, 10)]
+        + scratch,
         compiler_params=pltpu.CompilerParams(
             collective_id=0, has_side_effects=True, vmem_limit_bytes=67043328
         ),

time: 129 us -> 123 us (0.953)
  Pallas kernels: 128 us -> 122 us
    pallas_call x1, Pallas kernels: 124 us -> 117 us  [on_device(): pl.pallas_call(functools.partial(kernel, sizes), out_shape=shapes, in_spe...]
where the time goes in v3:
time: 123 us; the launch traced here: 122 us
  Pallas kernels  122 us (99%)
    pallas_call x1, Pallas kernels, on_device(): pl.pallas_call(functools.partial(kernel, sizes), out_shape=shapes, in_spe...  117 us
    pallas_call x1, Pallas kernels, hand_out(): pl.pallas_call(body, out_shape=[jax.ShapeDtypeStruct(array.shape[1:] if n...  4.37 us

profile of v3, /device:TPU:0, one launch (start us, length us, event | category | flops | bytes accessed | tf_op | source)
XLA Modules:
  0.0 122.4 jit_solution(7321165551056404181)
XLA Ops:
  0.6 117.2 %layer.1 = (bf16[256,1024]{1,0:T(8,128)(2,1)}, f32[256,1024]{1,0:T(8,128)}, f32[1,1024]{1,0:T(1,128)}, f32[1,1024]{1,0:T(1,128)}, f32[64,1536]{1,0:T(8,128)}, /*...) custom-call(bf16[256,1024]{1,0:T(8,128)(2,1)} %tokens_hbm.1, ...), custom_call_target="tpu_custom_call" | custom-call | tf_op jit(solution)/shard_map/layer/pallas_call | solution.py:1430
  117.9 4.4 %hand_out.1 = (bf16[256,1024]{1,0:T(8,128)(2,1)}, f32[256,1024]{1,0:T(8,128)}, f32[1024]{0:T(1024)}, f32[1024]{0:T(1024)}, f32[64,1536]{1,0:T(8,128)}, /*index=5...) custom-call(bf16[256,1024]{1,0:T(8,128)(2,1)} %get-tuple-element.35., ...), custom_call_target="tpu_custom_call" | custom-call | tf_op jit(solution)/shard_map/hand_out/pallas_call | solution.py:1304

commit v4 on v3

--- a/solution.py
+++ b/solution.py
@@ -146,10 +146,8 @@
     pass_recv,
     gx_send,
     gx_recv,
-    gu_send,
-    gu_recv,
-    gd_send,
-    gd_recv,
+    g_send,
+    g_recv,
     fin_send,
     fin_recv,
     half_send,
@@ -200,6 +198,9 @@
     def other_t(k):
         return lax.rem(t + k, nt)
 
+    def step_of(src, tt):
+        return lax.rem(tt - src + nt, nt) - 1
+
     def rows_at(start, size):
         return pl.ds(pl.multiple_of(start, size), size)
 
@@ -277,14 +278,14 @@
 
     def give_part(i, jj):
         dst = weights(i).at[own_rows]
-        return copy(part_of(i, jj), dst, share_send.at[i, jj], share_recv.at[i, j], member(jj))
+        return copy(part_of(i, jj), dst, share_send.at[i], share_recv.at[i], member(jj))
+
+    def all_parts(i):
+        rows = weights(i).at[pl.ds(0, (members - 1) * r)]
+        return copy(rows, rows, share_send.at[i], share_recv.at[i], partner)
 
     def member_rows(jj):
         return rows_at(z * zb + (jj % 2 * 2 + jj // 2) * r if gx == 2 else (x * nz + z) * chip + jj * r, r)
-
-    def take_part(i, jj):
-        dst = weights(i).at[member_rows(jj)]
-        return copy(part_of(i, j), dst, share_send.at[i, jj], share_recv.at[i, jj], member(jj))
 
     def share(i):
         local_copy(i).start()
@@ -296,10 +297,11 @@
         return padded(jnp.concatenate([array[:, a : a + HEAD] for a in at], axis=1))
 
     def own_doc(jj):
-        return copy(docs.at[j], docs.at[j], share_send.at[count, jj], share_recv.at[count, j], member(jj))
-
-    def doc_of(jj):
-        return copy(docs.at[jj], docs.at[jj], share_send.at[count, jj], share_recv.at[count, jj], member(jj))
+        return copy(docs.at[j], docs.at[j], share_send.at[count], share_recv.at[count], member(jj))
+
+    def all_docs():
+        rows = docs.at[pl.ds(0, members - 1)]
+        return copy(rows, rows, share_send.at[count], share_recv.at[count], partner)
 
     def stage():
         reads[0].wait()
@@ -371,7 +373,7 @@
 
     def act_turn(a, tt, src):
         b = acts[a].at[act_rows(j, src)]
-        return copy(b, b, turn_send.at[a, tt], turn_recv.at[a, src], turned(tt))
+        return copy(b, b, turn_send.at[a, step_of(src, tt)], turn_recv.at[a, step_of(src, tt)], turned(tt))
 
     def act_side(a, jj):
         b = acts[a].at[act_rows(jj, t)]
@@ -379,15 +381,15 @@
 
     def act_corner_x(a, jj, tt):
         b = acts[a].at[act_rows(jj, tt), over_x]
-        return copy(b, b, corner_x_send.at[a, tt], corner_x_recv.at[a, tt], across)
+        return copy(b, b, corner_x_send.at[a, step_of(t, tt)], corner_x_recv.at[a, step_of(t, tt)], across)
 
     def act_corner_t(a, tt, src):
         b = acts[a].at[act_rows(across_j, src), over_t]
-        return copy(b, b, corner_t_send.at[a, tt], corner_t_recv.at[a, src], turned(tt))
+        return copy(b, b, corner_t_send.at[a, step_of(src, tt)], corner_t_recv.at[a, step_of(src, tt)], turned(tt))
 
     def act_pass(a, jj, tt):
         b = acts[a].at[act_rows(jj, tt)]
-        return copy(b, b, pass_send.at[a, jj, tt], pass_recv.at[a, jj, tt], partner)
+        return copy(b, b, pass_send.at[a, jj % gx, tt], pass_recv.at[a, jj % gx, tt], partner)
 
     def act_start_side(a):
         if gx == 2:
@@ -450,11 +452,11 @@
 
     def send_up(i, src):
         b = w_block(i, src)
-        return copy(b, b, up_send.at[i, src], z_recv.at[i, src], along(z + 1))
+        return copy(b, b, up_send.at[i], z_recv.at[i, src], along(z + 1))
 
     def send_down(i, src):
         b = w_block(i, src)
-        return copy(b, b, down_send.at[i, src], z_recv.at[i, src], along(z - 1))
+        return copy(b, b, down_send.at[i], z_recv.at[i, src], along(z - 1))
 
     def send_across(i, src, xx):
         b = weights(i).at[rows_at((xx * nz + src) * chip, chip)]
@@ -462,20 +464,20 @@
 
     def send_first(i):
         def along_z(sems, to):
-            return copy(part_of(i, j), weights(i).at[own_rows], sems.at[i, z], z_recv.at[i, z], to)
+            return copy(part_of(i, j), weights(i).at[own_rows], sems.at[i], z_recv.at[i, z], to)
 
         pl.when(z < nz - 1)(lambda: along_z(up_send, along(z + 1)).start())
         pl.when(z > 0)(lambda: along_z(down_send, along(z - 1)).start())
 
     def send_own(i):
         local_copy(i).wait()
+        all_parts(i).wait_recv()
         for k in range(1, members):
             jj = other_j(k)
-            take_part(i, jj).wait_recv()
             rows = weights(i).at[member_rows(jj)]
 
             def along_z(sems, to):
-                return copy(rows, rows, sems.at[i, z], z_recv.at[i, z], to)
+                return copy(rows, rows, sems.at[i], z_recv.at[i, z], to)
 
             pl.when(z < nz - 1)(lambda: along_z(up_send, along(z + 1)).start())
             pl.when(z > 0)(lambda: along_z(down_send, along(z - 1)).start())
@@ -521,8 +523,8 @@
         return copy(
             of(zs_a, zs_u, zs_d, i).at[b],
             of(zu_a, zu_u, zu_d, i).at[b],
-            gu_send.at[i, to_z],
-            gu_recv.at[i, to_z],
+            g_send.at[i],
+            g_recv.at[i, to_z + 1],
             along(z + 1),
         )
 
@@ -531,8 +533,8 @@
         return copy(
             of(zs_a, zs_u, zs_d, i).at[b],
             of(zd_a, zd_u, zd_d, i).at[b],
-            gd_send.at[i, to_z],
-            gd_recv.at[i, to_z],
+            g_send.at[i],
+            g_recv.at[i, to_z],
             along(z - 1),
         )
 
@@ -541,10 +543,18 @@
         return copy(
             of(fs_a, fs_u, fs_d, i).at[rows_at(at, r)],
             of(fr_a, fr_u, fr_d, i).at[src],
-            fin_send.at[i, jj],
-            fin_recv.at[i, src],
+            fin_send.at[i],
+            fin_recv.at[i],
             member(jj),
         )
+
+    def all_given(i):
+        rows = of(fs_a, fs_u, fs_d, i).at[pl.ds(0, (members - 1) * r)]
+        return copy(rows, rows, fin_send.at[i], fin_recv.at[i], partner)
+
+    def all_taken(i):
+        rows = of(fr_a, fr_u, fr_d, i).at[pl.ds(0, members - 1)]
+        return copy(rows, rows, fin_send.at[i], fin_recv.at[i], partner)
 
     def products(i, columns):
         if i in A:
@@ -630,8 +640,7 @@
             g_final(i, other_j(k), j).start()
 
     def finish(i):
-        for k in range(1, members):
-            g_final(i, j, other_j(k)).wait_recv()
+        all_taken(i).wait_recv()
         keep = own_of(i)[rows_at(z * zb + own_index() * r, r), :]
         came = of(fr_a, fr_u, fr_d, i)
         for jj in range(members):
@@ -682,8 +691,7 @@
         lax.fori_loop(0, length // 128, table, 0)
 
     def prepare_docs():
-        for k in range(1, members):
-            doc_of(other_j(k)).wait_recv()
+        all_docs().wait_recv()
         for s in range(members):
             for n in range(length // 128):
                 cut = slice(n * 128, (n + 1) * 128)
@@ -850,11 +858,13 @@
 
     def corner_t_copy(a, tt, src):
         b = partials[a].at[block_rows(across_j, tt), back_t]
-        return copy(b, corner_t.at[a % nbuf, src], corner_t_send.at[2 + a, tt], corner_t_recv.at[2 + a, src], turned(tt))
+        n = step_of(src, tt)
+        return copy(b, corner_t.at[a % nbuf, src], corner_t_send.at[2 + a, n], corner_t_recv.at[2 + a, n], turned(tt))
 
     def corner_x_copy(a, jj, tt):
         b = partials[a].at[block_rows(jj, tt), back_x]
-        return copy(b, corner_x.at[a % nbuf, tt], corner_x_send.at[2 + a, tt], corner_x_recv.at[2 + a, tt], across)
+        n = step_of(t, tt)
+        return copy(b, corner_x.at[a % nbuf, tt], corner_x_send.at[2 + a, n], corner_x_recv.at[2 + a, n], across)
 
     def side_copy(a, jj):
         b = partials[a].at[block_rows(jj, t)]
@@ -862,7 +872,8 @@
 
     def turn_copy(a, tt, src):
         b = partials[a].at[block_rows(j, tt)]
-        return copy(b, side_t.at[a % nbuf, src], turn_send.at[2 + a, tt], turn_recv.at[2 + a, src], turned(tt))
+        n = step_of(src, tt)
+        return copy(b, side_t.at[a % nbuf, src], turn_send.at[2 + a, n], turn_recv.at[2 + a, n], turned(tt))
 
     def reduce_corner(a):
         if gx == 2:
@@ -988,12 +999,20 @@
 
     def peer_copy(to, src):
         device_to = device(to, x, c, t) if gx == 2 else device(to // 2, to % 2, c, t)
-        return copy(vec_z.at[peer], vec_z.at[src], peer_send.at[to], peer_recv.at[src], device_to)
+        return copy(vec_z.at[peer], vec_z.at[src], peer_send.at[0], peer_recv.at[0], device_to)
 
     def mate_copy(to, src):
         jj, tt = to // nt, to % nt
         device_to = device(z, jj % 2, jj // 2, tt) if gx == 2 else device(z, x, jj, tt)
-        return copy(vec_m.at[mate], vec_m.at[src], mate_send.at[to], mate_recv.at[src], device_to)
+        return copy(vec_m.at[mate], vec_m.at[src], mate_send.at[0], mate_recv.at[0], device_to)
+
+    def all_peers():
+        rows = vec_z.at[pl.ds(0, peers - 1)]
+        return copy(rows, rows, peer_send.at[0], peer_recv.at[0], partner)
+
+    def all_mates():
+        rows = vec_m.at[pl.ds(0, mates - 1)]
+        return copy(rows, rows, mate_send.at[0], mate_recv.at[0], partner)
 
     def sums_start():
         vec_z[peer] = vec[...]
@@ -1001,8 +1020,7 @@
             peer_copy(lax.rem(peer + k, peers), peer).start()
 
     def sums_group():
-        for k in range(1, peers):
-            peer_copy(peer, lax.rem(peer + k, peers)).wait_recv()
+        all_peers().wait_recv()
         total = vec_z[0]
         for k in range(1, peers):
             total = total + vec_z[k]
@@ -1011,8 +1029,7 @@
             mate_copy(lax.rem(mate + k, mates), mate).start()
 
     def sums_end():
-        for k in range(1, mates):
-            mate_copy(mate, lax.rem(mate + k, mates)).wait_recv()
+        all_mates().wait_recv()
         total = vec_m[0]
         for k in range(1, mates):
             total = total + vec_m[k]
@@ -1029,10 +1046,8 @@
                 qkv_bias[:, 3 * at : 3 * (at + wide)] = jnp.concatenate(heads, axis=1)
 
     def sums_sent():
-        for k in range(1, peers):
-            peer_copy(lax.rem(peer + k, peers), peer).wait_send()
-        for k in range(1, mates):
-            mate_copy(lax.rem(mate + k, mates), mate).wait_send()
+        all_peers().wait_send()
+        all_mates().wait_send()
 
     def forwards(some, lo, hi):
         for d in range(lo, hi):
@@ -1258,19 +1273,23 @@
         any_order()
 
     for i in range(count):
-        for k in range(1, members):
-            g_final(i, other_j(k), j).wait_send()
-            give_part(i, other_j(k)).wait_send()
-        for src in range(nz):
-            pl.when((z < nz - 1) & (src <= z))(lambda: send_up(i, src).wait_send())
-            pl.when((z > 0) & (src >= z))(lambda: send_down(i, src).wait_send())
-            pl.when(src > z)(lambda: g_up(i, src).wait_send())
-            pl.when(src < z)(lambda: g_down(i, src).wait_send())
-            if gx == 1:
+        all_given(i).wait_send()
+        all_parts(i).wait_send()
+        for n in range(1, nz):
+            blocks = weights(i).at[pl.ds(0, n * zb)]
+            pl.when(z == n - 1)(
+                lambda: copy(blocks, blocks, up_send.at[i], z_recv.at[i, 0], along(z + 1)).wait_send()
+            )
+            pl.when(z == nz - n)(
+                lambda: copy(blocks, blocks, down_send.at[i], z_recv.at[i, 0], along(z - 1)).wait_send()
+            )
+        sums = of(zs_a, zs_u, zs_d, i).at[pl.ds(0, (nz - 1) * zb)]
+        copy(sums, sums, g_send.at[i], g_recv.at[i, 0], partner).wait_send()
+        if gx == 1:
+            for src in range(nz):
                 send_across(i, src, x).wait_send()
                 g_across(i, src).wait_send()
-    for k in range(1, members):
-        own_doc(other_j(k)).wait_send()
+    all_docs().wait_send()
     reduce_sent(0)
     reduce_sent(1)
     sums_sent()
@@ -1347,7 +1366,7 @@
     pw = 512 if units % 512 == 0 else units
     nm = units // pw
     nbuf = gx
-    peers, mates = (nz if gx == 2 else 2 * nz), members * nt
+    peers, mates, steps = (nz if gx == 2 else 2 * nz), members * nt, max(nt - 1, 1)
     sizes = dict(nt=nt, nz=nz, gx=gx, na=na, nm=nm, hp=hp, length=length, R=R, r=r, pw=pw, nbuf=nbuf)
 
     widths = ((na, 512), (nm, pw), (nm, pw))
@@ -1381,17 +1400,18 @@
         + [V((n, gx * chip, w), BF16) for n, w in widths]
         + [V((n, members, r, w), BF16) for n, w in widths]
         + [V((8, D // 2), F32), V((peers, 8, D // 2), F32), V((mates, 8, D // 2), F32)]
-        + [DMA((count,)), DMA((10,)), DMA((count + 1, members)), DMA((count + 1, members))]
-        + [DMA((count, nz))] * 5
-        + [DMA((4, nt))] * 2
+        + [DMA((count,)), DMA((10,)), DMA((count + 1,)), DMA((count + 1,))]
+        + [DMA((count,)), DMA((count,)), DMA((count, nz))]
+        + [DMA((count, nz) if gx == 1 else (1, 1))] * 2
+        + [DMA((4, steps))] * 2
         + [DMA((4,))] * 2
-        + [DMA((4, nt))] * 4
-        + [DMA((2, members, nt))] * 2
-        + [DMA((count, nz))] * 6
-        + [DMA((count, members))] * 2
+        + [DMA((4, steps))] * 4
+        + [DMA((2, gx, nt))] * 2
+        + [DMA((count, nz) if gx == 1 else (1, 1))] * 2
+        + [DMA((count,)), DMA((count, nz + 1))]
+        + [DMA((count,))] * 2
         + [DMA((2, gx))] * 2
-        + [DMA((peers,))] * 2
-        + [DMA((mates,))] * 2
+        + [DMA((1,))] * 4
         + [pltpu.SemaphoreType.REGULAR((2,))]
     )
     space, far = pl.BlockSpec(memory_space=pltpu.VMEM), pl.BlockSpec(memory_space=pl.ANY)

time: 123 us -> 121 us (0.984)
  Pallas kernels: 122 us -> 120 us
    pallas_call x1, Pallas kernels: 117 us -> 116 us  [on_device(): pl.pallas_call(functools.partial(kernel, sizes), out_shape=shapes, in_spe...]
where the time goes in v4:
time: 121 us
  Pallas kernels  120 us (99%)
    pallas_call x1, Pallas kernels, on_device(): pl.pallas_call(functools.partial(kernel, sizes), out_shape=shapes, in_spe...  116 us
    pallas_call x1, Pallas kernels, hand_out(): pl.pallas_call(body, out_shape=[jax.ShapeDtypeStruct(array.shape[1:] if n...  4.37 us

profile of v4, /device:TPU:0, one launch (start us, length us, event | category | flops | bytes accessed | tf_op | source)
XLA Modules:
  0.0 120.7 jit_solution(1732134364755892016)
XLA Ops:
  0.6 115.5 %layer.1 = (bf16[256,1024]{1,0:T(8,128)(2,1)}, f32[256,1024]{1,0:T(8,128)}, f32[1,1024]{1,0:T(1,128)}, f32[1,1024]{1,0:T(1,128)}, f32[64,1536]{1,0:T(8,128)}, /*...) custom-call(bf16[256,1024]{1,0:T(8,128)(2,1)} %tokens_hbm.1, ...), custom_call_target="tpu_custom_call" | custom-call | tf_op jit(solution)/shard_map/layer/pallas_call | solution.py:1450
  116.2 4.4 %hand_out.1 = (bf16[256,1024]{1,0:T(8,128)(2,1)}, f32[256,1024]{1,0:T(8,128)}, f32[1024]{0:T(1024)}, f32[1024]{0:T(1024)}, f32[64,1536]{1,0:T(8,128)}, /*index=5...) custom-call(bf16[256,1024]{1,0:T(8,128)(2,1)} %get-tuple-element.35., ...), custom_call_target="tpu_custom_call" | custom-call | tf_op jit(solution)/shard_map/hand_out/pallas_call | solution.py:1323

commit v5 on v4

--- a/solution.py
+++ b/solution.py
@@ -38,37 +38,49 @@
     sizes,
     tokens_hbm,
     cotangent_hbm,
+    segments_hbm,
+    gain_hbm,
+    shift_hbm,
+    w_qkv_hbm,
+    b_qkv_hbm,
+    w_dense_hbm,
+    b_dense_hbm,
+    w_up,
+    b_up_hbm,
+    w_down,
+    b_down_hbm,
+    output_hbm,
+    input_grad_hbm,
+    gain_grad_hbm,
+    shift_grad_hbm,
+    qkv_grad_hbm,
+    qkv_bias_hbm,
+    dense_grad_hbm,
+    dense_bias_hbm,
+    up_grad_hbm,
+    up_bias_hbm,
+    down_grad_hbm,
+    tokens,
+    cotangent,
     segments,
     gain,
     shift,
-    w_qkv_hbm,
+    w_qkv,
     b_qkv,
-    w_dense_hbm,
+    w_dense,
     b_dense,
-    w_up,
     b_up,
-    w_down,
     b_down,
-    output_hbm,
-    input_grad_hbm,
+    output,
+    input_grad,
     gain_grad,
     shift_grad,
-    qkv_grad_hbm,
+    qkv_grad,
     qkv_bias,
-    dense_grad_hbm,
+    dense_grad,
     dense_bias,
-    up_grad_hbm,
+    up_grad,
     up_bias,
-    down_grad_hbm,
-    tokens,
-    cotangent,
-    w_qkv,
-    w_dense,
-    output,
-    input_grad,
-    qkv_grad,
-    dense_grad,
-    up_grad,
     down_grad,
     wa_in,
     ba,
@@ -246,7 +258,19 @@
     reads = [
         pltpu.make_async_copy(src, dst, io_sem.at[n])
         for n, (src, dst) in enumerate(
-            ((w_qkv_hbm, w_qkv), (w_dense_hbm, w_dense), (tokens_hbm, tokens), (cotangent_hbm, cotangent))
+            (
+                (segments_hbm, segments),
+                (gain_hbm, gain),
+                (shift_hbm, shift),
+                (b_qkv_hbm, b_qkv),
+                (b_dense_hbm, b_dense),
+                (b_up_hbm, b_up),
+                (b_down_hbm, b_down),
+                (w_qkv_hbm, w_qkv),
+                (w_dense_hbm, w_dense),
+                (tokens_hbm, tokens),
+                (cotangent_hbm, cotangent),
+            )
         )
     ]
     for read in reads:
@@ -262,10 +286,15 @@
         (dense_grad, dense_grad_hbm),
         (up_grad, up_grad_hbm),
         (down_grad, down_grad_hbm),
+        (gain_grad, gain_grad_hbm),
+        (shift_grad, shift_grad_hbm),
+        (qkv_bias, qkv_bias_hbm),
+        (dense_bias, dense_bias_hbm),
+        (up_bias, up_bias_hbm),
     )
 
     def result(n):
-        return pltpu.make_async_copy(*results[n], io_sem.at[4 + n])
+        return pltpu.make_async_copy(*results[n], io_sem.at[11 + n])
 
     def part_of(i, jj):
         if i in A:
@@ -304,8 +333,8 @@
         return copy(rows, rows, share_send.at[count], share_recv.at[count], partner)
 
     def stage():
-        reads[0].wait()
-        reads[1].wait()
+        for read in reads[:9]:
+            read.wait()
         for jj in range(members):
             for k in range(na):
                 for part in range(3):
@@ -350,7 +379,7 @@
     near = (j, partner_j, across_j, far_j)
 
     def fill_normed():
-        reads[2].wait()
+        reads[9].wait()
 
         def body(n, carry):
             rows = rows_at(n * tile, tile)
@@ -363,7 +392,7 @@
         lax.fori_loop(0, R // tile, body, 0)
 
     def fill_grads():
-        reads[3].wait()
+        reads[10].wait()
 
         def body(n, carry):
             grads[rows_at((j * nt + t) * R + n * tile, tile), :] = permute(cotangent[rows_at(n * tile, tile), :])
@@ -1044,6 +1073,8 @@
                 heads = [part[:, p * 128 + h * HEAD : p * 128 + (h + 1) * HEAD] for h in range(hp) for p in range(3)]
                 at = (jj * na + k) * wide
                 qkv_bias[:, 3 * at : 3 * (at + wide)] = jnp.concatenate(heads, axis=1)
+        for n in range(6, 11):
+            result(n).start()
 
     def sums_sent():
         all_peers().wait_send()
@@ -1298,38 +1329,45 @@
 
 
 def hand_out(arrays):
-    wide = [n for n, array in enumerate(arrays) if array.shape[0] > 1]
-    thin = [n for n, array in enumerate(arrays) if array.shape[0] == 1]
+    count = len(arrays)
+    thin = [array.shape[0] == 1 for array in arrays]
+    leaving = [
+        jax.ShapeDtypeStruct(array.shape[1:] if flat else array.shape, array.dtype) for array, flat in zip(arrays, thin)
+    ]
 
     def body(*refs):
-        count = len(arrays)
-        given, taken, buffers, sems = refs[:count], refs[count : 2 * count], refs[2 * count : -1], refs[-1]
-        reads = [pltpu.make_async_copy(given[n], buffers[i], sems.at[0, i]) for i, n in enumerate(wide)]
-        writes = [pltpu.make_async_copy(buffers[i], taken[n], sems.at[1, i]) for i, n in enumerate(wide)]
-        for read in reads:
-            read.start()
-        for n in thin:
-            taken[n][...] = given[n][0]
-        for read, write in zip(reads, writes):
-            read.wait()
-            write.start()
-        for write in writes:
-            write.wait()
-
-    def specs():
-        return [pl.BlockSpec(memory_space=pltpu.VMEM if n in thin else pl.ANY) for n in range(len(arrays))]
-
+        given, taken, came, goes, sems = (
+            refs[:count],
+            refs[count : 2 * count],
+            refs[2 * count : 3 * count],
+            refs[3 * count : -1],
+            refs[-1],
+        )
+        reads = [pltpu.make_async_copy(given[n], came[n], sems.at[0, n]) for n in range(count)]
+        writes = [
+            pltpu.make_async_copy(goes[n] if thin[n] else came[n], taken[n], sems.at[1, n]) for n in range(count)
+        ]
+        order = sorted(range(count), key=lambda n: thin[n])
+        for n in order:
+            reads[n].start()
+        for n in order:
+            reads[n].wait()
+            if thin[n]:
+                goes[n][...] = came[n][0]
+            writes[n].start()
+        for n in order:
+            writes[n].wait()
+
+    far = pl.BlockSpec(memory_space=pl.ANY)
     return list(
         pl.pallas_call(
             body,
-            out_shape=[
-                jax.ShapeDtypeStruct(array.shape[1:] if n in thin else array.shape, array.dtype)
-                for n, array in enumerate(arrays)
-            ],
-            in_specs=specs(),
-            out_specs=specs(),
-            scratch_shapes=[pltpu.VMEM(arrays[n].shape, arrays[n].dtype) for n in wide]
-            + [pltpu.SemaphoreType.DMA((2, len(wide)))],
+            out_shape=leaving,
+            in_specs=[far] * count,
+            out_specs=[far] * count,
+            scratch_shapes=[pltpu.VMEM(array.shape, array.dtype) for array in arrays]
+            + [pltpu.VMEM(part.shape if flat else (8, 128), part.dtype) for part, flat in zip(leaving, thin)]
+            + [pltpu.SemaphoreType.DMA((2, count))],
             name="hand_out",
         )(*arrays)
     )
@@ -1400,7 +1438,7 @@
         + [V((n, gx * chip, w), BF16) for n, w in widths]
         + [V((n, members, r, w), BF16) for n, w in widths]
         + [V((8, D // 2), F32), V((peers, 8, D // 2), F32), V((mates, 8, D // 2), F32)]
-        + [DMA((count,)), DMA((10,)), DMA((count + 1,)), DMA((count + 1,))]
+        + [DMA((count,)), DMA((22,)), DMA((count + 1,)), DMA((count + 1,))]
         + [DMA((count,)), DMA((count,)), DMA((count, nz))]
         + [DMA((count, nz) if gx == 1 else (1, 1))] * 2
         + [DMA((4, steps))] * 2
@@ -1414,7 +1452,7 @@
         + [DMA((1,))] * 4
         + [pltpu.SemaphoreType.REGULAR((2,))]
     )
-    space, far = pl.BlockSpec(memory_space=pltpu.VMEM), pl.BlockSpec(memory_space=pl.ANY)
+    far = pl.BlockSpec(memory_space=pl.ANY)
 
     def row(vector):
         return vector.reshape(1, -1)
@@ -1450,10 +1488,10 @@
     out = pl.pallas_call(
         functools.partial(kernel, sizes),
         out_shape=shapes,
-        in_specs=[far if n in (0, 1, 5, 7, 9, 11) else space for n in range(len(args))],
-        out_specs=[space if n in (2, 3, 5, 7, 9) else far for n in range(len(shapes))],
-        scratch_shapes=[V(args[n].shape, BF16) for n in (0, 1, 5, 7)]
-        + [V(shapes[n].shape, shapes[n].dtype) for n in (0, 1, 4, 6, 8, 10)]
+        in_specs=[far] * len(args),
+        out_specs=[far] * len(shapes),
+        scratch_shapes=[V(args[n].shape, args[n].dtype) for n in (0, 1, 2, 3, 4, 5, 6, 7, 8, 10, 12)]
+        + [V(shape.shape, shape.dtype) for shape in shapes]
         + scratch,
         compiler_params=pltpu.CompilerParams(
             collective_id=0, has_side_effects=True, vmem_limit_bytes=67043328

time: 121 us -> 119 us (0.983)
  Pallas kernels: 120 us -> 117 us
    pallas_call x1, Pallas kernels: 4.37 us -> 3.1 us  [hand_out(): pl.pallas_call(body, out_shape=leaving, in_specs=[far] * count, out_specs...]
where the time goes in v5:
time: 119 us; the launch traced here: 118 us
  Pallas kernels  117 us (98%)
    pallas_call x1, Pallas kernels, on_device(): pl.pallas_call(functools.partial(kernel, sizes), out_shape=shapes, in_spe...  114 us
    pallas_call x1, Pallas kernels, hand_out(): pl.pallas_call(body, out_shape=leaving, in_specs=[far] * count, out_specs...  3.1 us

profile of v5, /device:TPU:0, one launch (start us, length us, event | category | flops | bytes accessed | tf_op | source)
XLA Modules:
  0.0 118.3 jit_solution(8993898836740733983)
XLA Ops:
  0.6 114.4 %layer.1 = (bf16[256,1024]{1,0:T(8,128)(2,1)}, f32[256,1024]{1,0:T(8,128)}, f32[1,1024]{1,0:T(1,128)}, f32[1,1024]{1,0:T(1,128)}, f32[64,1536]{1,0:T(8,128)}, /*...) custom-call(bf16[256,1024]{1,0:T(8,128)(2,1)} %tokens_hbm.1, ...), custom_call_target="tpu_custom_call" | custom-call | tf_op jit(solution)/shard_map/layer/pallas_call | solution.py:1488
  115.1 3.1 %hand_out.1 = (bf16[256,1024]{1,0:T(8,128)(2,1)}, f32[256,1024]{1,0:T(8,128)}, f32[1024]{0:T(1024)}, f32[1024]{0:T(1024)}, f32[64,1536]{1,0:T(8,128)}, /*index=5...) custom-call(bf16[256,1024]{1,0:T(8,128)(2,1)} %get-tuple-element.35., ...), custom_call_target="tpu_custom_call" | custom-call | tf_op jit(solution)/shard_map/hand_out/pallas_call | solution.py:1363

commit v6 on v5

--- a/solution.py
+++ b/solution.py
@@ -984,15 +984,16 @@
         result(0).start()
 
     def put(row, at, values):
+        at += row * D
         end = at + values.shape[1]
-        for h in range(2):
+        for h in range(vec.shape[0]):
             lo, hi = max(at, h * D // 2), min(end, (h + 1) * D // 2)
             if lo < hi:
                 cols = slice(lo - h * D // 2, hi - h * D // 2)
-                vec[2 * row + h : 2 * row + h + 1, cols] += values[:, lo - at : hi - at]
-
-    def taken(array, row):
-        return jnp.concatenate([array[2 * row : 2 * row + 1], array[2 * row + 1 : 2 * row + 2]], axis=1)
+                vec[h : h + 1, cols] += values[:, lo - at : hi - at]
+
+    def taken(array, row, count=2):
+        return jnp.concatenate([array[2 * row + h : 2 * row + h + 1] for h in range(count)], axis=1)
 
     def sum_biases():
         vec[...] = jnp.zeros_like(vec)
@@ -1066,7 +1067,7 @@
         shift_grad[...] = taken(total, 1)
         dense_bias[...] = taken(total, 2)
         for jj in range(members):
-            row = taken(vec_m[jj * nt + t], 3)
+            row = taken(vec_m[jj * nt + t], 3, vec.shape[0] - 6)
             up_bias[:, jj * units : (jj + 1) * units] = row[:, :units]
             for k in range(na):
                 part = row[:, units + k * 384 : units + (k + 1) * 384]
@@ -1179,124 +1180,124 @@
         enter()
         share(a)
         give_docs()
+        send_first(a)
         send_first(d)
+        share(u)
+        send_first(u)
+        fill_grads()
         fill_normed()
-        send_first(u)
-        share(u)
-        prepare()
-        send_first(a)
-        fill_grads()
         act_start_turn(0)
         send_own(a)
         act_start_side(0)
         act_start_side(1)
-        act_start_turn(1)
+        share(d)
         send_own(u)
         forward_up(a, 1)
-        share(d)
         forward_down(a, 1)
+        prepare()
+        prepare_docs()
+        act_start_turn(1)
+        forward_up(u, 1)
         forward_down(u, 1)
         forward_down(a, 2)
-        forward_up(u, 1)
-        prepare_docs()
+        act_from_side(0)
+        act_from_turn(0)
         forward_up(a, 2)
-        act_from_turn(0)
-        act_from_side(0)
         act_wait_of(0, partner_j)
-        forward_down(u, 2)
         forward_up(u, 2)
         forward_up(a, 3)
         forward_down(a, 3)
+        act_from_turn(1)
+        forward_down(u, 2)
+        project(0, partner_j)
         act_from_side(1)
-        act_from_turn(1)
-        project(0, partner_j)
+        act_wait_of(1, partner_j)
         send_own(d)
+        project_back(0, partner_j)
+        project(0, j)
         project_back(0, j)
-        project(0, j)
-        attend(0, j)
-        act_wait_of(1, partner_j)
+        attend(0, partner_j)
         act_finish(0)
+        forward_up(u, 3)
         forward_down(u, 3)
-        forward_up(u, 3)
+        project(0, across_j)
         hidden(0, across_j)
         hidden(0, j)
+        hidden(0, partner_j)
         act_wait_of(0, far_j)
-        hidden(0, partner_j)
+        forward_down(d, 1)
+        forward_up(d, 1)
+        act_finish(1)
         hidden(0, far_j)
-        act_finish(1)
-        forward_up(d, 1)
-        forward_down(d, 1)
-        project(0, across_j)
         project(0, far_j)
+        project_back(0, across_j)
         act_wait_of(1, far_j)
+        weight_grad_cut(d, 1)
+        chain_up(d, 0)
         weight_grad_cut(d, 0)
         chain_down(d, 0)
-        weight_grad_cut(d, 1)
-        chain_up(d, 0)
         project_back(0, far_j)
-        attend(0, far_j)
-        project_back(0, across_j)
+        attend(0, j)
         forward_up(d, 2)
         forward_down(d, 2)
         attend(0, across_j)
+        chain_up(d, 1)
         chain_down(d, 1)
-        project_back(0, partner_j)
-        chain_up(d, 1)
-        attend(0, partner_j)
+        attend(0, far_j)
+        forward_up(d, 3)
         forward_down(d, 3)
-        forward_up(d, 3)
+        hidden_back(0, across_j)
         hidden_back(0, far_j)
         branch_give(1, far_j)
-        hidden_back(0, across_j)
+        chain_up(d, 2)
         chain_down(d, 2)
-        chain_up(d, 2)
         branch(1, across_j)
+        weight_grad_cut(a, 0)
         reduce_corner(1)
-        weight_grad_cut(a, 0)
         weight_grad_cut(a, 1)
         chain_down(a, 0)
         chain_up(a, 0)
+        hidden_back(0, j)
         act_sent(0)
         act_sent(1)
         branch_give(0, far_j)
-        hidden_back(0, j)
         hidden_back(0, partner_j)
+        weight_grad_cut(u, 1)
+        chain_end(d)
+        chain_up(u, 0)
+        weight_grad_cut(u, 0)
+        chain_down(u, 0)
         branch(0, across_j)
-        weight_grad_cut(u, 0)
         reduce_corner(0)
-        chain_down(u, 0)
-        weight_grad_cut(u, 1)
-        chain_up(u, 0)
-        sum_biases()
-        chain_end(d)
         chain_up(a, 1)
         reduce_side(1)
-        branch(1, j)
-        branch_give(1, partner_j)
         chain_down(a, 1)
         branch(0, j)
-        reduce_turn(1)
+        branch_give(1, partner_j)
+        branch(1, j)
+        finish(d)
         branch_give(0, partner_j)
         chain_up(u, 1)
+        reduce_turn(1)
         chain_down(u, 1)
-        finish(d)
+        chain_down(a, 2)
+        chain_up(a, 2)
         reduce_side(0)
         reduce_turn(0)
-        chain_up(a, 2)
-        chain_down(a, 2)
+        chain_up(u, 2)
+        chain_down(u, 2)
+        sum_biases()
         reduce_wait(1)
         write_input_grad()
+        chain_end(a)
         sums_start()
-        chain_down(u, 2)
-        chain_up(u, 2)
-        chain_end(a)
+        chain_end(u)
         sums_group()
-        chain_end(u)
-        sums_end()
+        finish(u)
+        finish(a)
         reduce_wait(0)
         write_output()
-        finish(a)
-        finish(u)
+        sums_end()
 
     if (gx, na, nm, nz, tiles, RT) == (2, 1, 1, 4, 4, length):
         tuned_order()
@@ -1412,6 +1413,7 @@
     rows = members * length
     own = D if gx == 2 else D // 2
     chip = 2 * r
+    small = -(-(6 * (D // 2) + units + na * 384) // (4 * D)) * 8
     split = D // 4
     V = pltpu.VMEM
     DMA = pltpu.SemaphoreType.DMA
@@ -1437,7 +1439,7 @@
         + [V((n, own, w), BF16) for _ in range(3) for n, w in widths]
         + [V((n, gx * chip, w), BF16) for n, w in widths]
         + [V((n, members, r, w), BF16) for n, w in widths]
-        + [V((8, D // 2), F32), V((peers, 8, D // 2), F32), V((mates, 8, D // 2), F32)]
+        + [V((small, D // 2), F32), V((peers, small, D // 2), F32), V((mates, small, D // 2), F32)]
         + [DMA((count,)), DMA((22,)), DMA((count + 1,)), DMA((count + 1,))]
         + [DMA((count,)), DMA((count,)), DMA((count, nz))]
         + [DMA((count, nz) if gx == 1 else (1, 1))] * 2

time: 119 us -> 118 us (level)
  no operation moved by 1% of the time
where the time goes in v6:
time: 118 us; the launch traced here: 117 us
  Pallas kernels  117 us (99%)
    pallas_call x1, Pallas kernels, on_device(): pl.pallas_call(functools.partial(kernel, sizes), out_shape=shapes, in_spe...  113 us
    pallas_call x1, Pallas kernels, hand_out(): pl.pallas_call(body, out_shape=leaving, in_specs=[far] * count, out_specs...  3.1 us

profile of v6, /device:TPU:0, one launch (start us, length us, event | category | flops | bytes accessed | tf_op | source)
XLA Modules:
  0.0 117.4 jit_solution(14990690662853059901)
XLA Ops:
  0.6 113.5 %layer.1 = (bf16[256,1024]{1,0:T(8,128)(2,1)}, f32[256,1024]{1,0:T(8,128)}, f32[1,1024]{1,0:T(1,128)}, f32[1,1024]{1,0:T(1,128)}, f32[64,1536]{1,0:T(8,128)}, /*...) custom-call(bf16[256,1024]{1,0:T(8,128)(2,1)} %tokens_hbm.1, ...), custom_call_target="tpu_custom_call" | custom-call | tf_op jit(solution)/shard_map/layer/pallas_call | solution.py:1490
  114.2 3.1 %hand_out.1 = (bf16[256,1024]{1,0:T(8,128)(2,1)}, f32[256,1024]{1,0:T(8,128)}, f32[1024]{0:T(1024)}, f32[1024]{0:T(1024)}, f32[64,1536]{1,0:T(8,128)}, /*index=5...) custom-call(bf16[256,1024]{1,0:T(8,128)(2,1)} %get-tuple-element.35., ...), custom_call_target="tpu_custom_call" | custom-call | tf_op jit(solution)/shard_map/hand_out/pallas_call | solution.py:1364

commit v7 on v6

--- a/solution.py
+++ b/solution.py
@@ -811,7 +811,7 @@
             value_sum[here_rows, :] += unstacked(dot(p, g, 0, 0))
             return carry
 
-        lax.fori_loop(0, length // block, body, 0)
+        lax.fori_loop(0, length // block, body, 0, unroll=2)
         rows = rows_at(s * length, length)
         grad_z[k, rows, 128:256] = rotated(key_sum[...], slice(None), -1.0).astype(BF16)
         grad_z[k, rows, 256:384] = value_sum[...].astype(BF16)

time: 118 us -> 117 us (level)
  no operation moved by 1% of the time
where the time goes in v7:
time: 117 us
  Pallas kernels  116 us (99%)
    pallas_call x1, Pallas kernels, on_device(): pl.pallas_call(functools.partial(kernel, sizes), out_shape=shapes, in_spe...  113 us
    pallas_call x1, Pallas kernels, hand_out(): pl.pallas_call(body, out_shape=leaving, in_specs=[far] * count, out_specs...  3.1 us

profile of v7, /device:TPU:0, one launch (start us, length us, event | category | flops | bytes accessed | tf_op | source)
XLA Modules:
  0.0 116.9 jit_solution(2047278559030238009)
XLA Ops:
  0.6 113.0 %layer.1 = (bf16[256,1024]{1,0:T(8,128)(2,1)}, f32[256,1024]{1,0:T(8,128)}, f32[1,1024]{1,0:T(1,128)}, f32[1,1024]{1,0:T(1,128)}, f32[64,1536]{1,0:T(8,128)}, /*...) custom-call(bf16[256,1024]{1,0:T(8,128)(2,1)} %tokens_hbm.1, ...), custom_call_target="tpu_custom_call" | custom-call | tf_op jit(solution)/shard_map/layer/pallas_call | solution.py:1490
  113.6 3.1 %hand_out.1 = (bf16[256,1024]{1,0:T(8,128)(2,1)}, f32[256,1024]{1,0:T(8,128)}, f32[1024]{0:T(1024)}, f32[1024]{0:T(1024)}, f32[64,1536]{1,0:T(8,128)}, /*index=5...) custom-call(bf16[256,1024]{1,0:T(8,128)(2,1)} %get-tuple-element.35., ...), custom_call_target="tpu_custom_call" | custom-call | tf_op jit(solution)/shard_map/hand_out/pallas_call | solution.py:1364
